TPU v7x, 256 devices: a whole 4x4x8 slice. The times are simulated.
256 devices in a mesh: group: 16 (over z_lo, y), fsdp: 16 (over x, z_hi, core).
Axes of the slice: x: 4, y: 4, z: 8 (z_hi: 2, z_lo: 4; z = z_hi * 4 + z_lo), core: 2. Of those that a mesh axis runs over, the one named last changes fastest.
Arguments:
- frames: bfloat16 [16, 8192, 1280], P('group', 'fsdp'), may hold values from -6 to 6
- cotangent: bfloat16 [16, 8192, 1280], P('group', 'fsdp'), may hold values from -12 to 12
- mix_partner: int32 [16, 64], P('group', 'fsdp'), may hold values from 0 to 3
- lengths: int32 [16, 64], P('group', 'fsdp'), may hold values from 32 to 128, as said below
- inner_params: bfloat16 [16, 1280, 2, 2560], P('group', 'fsdp'), may hold values from -6 to 6
- first_moment: float32 [16, 1280, 2, 2560], P('group', 'fsdp'), may hold values from -6 to 6
- second_moment: float32 [16, 1280, 2, 2560], P('group', 'fsdp'), may hold values from 0.25 to 4
- outer_params: float32 [1280, 2, 2560], P('fsdp'), may hold values from -6 to 6
- momentum: float32 [1280, 2, 2560], P('fsdp'), may hold values from -3 to 3
Outputs:
- new_moment: float32 [16, 1280, 2, 2560], P('group', 'fsdp')
- new_outer: float32 [1280, 2, 2560], P('fsdp')
- new_momentum: float32 [1280, 2, 2560], P('fsdp')
Inputs may be any that keep to these rules, and one draw needn't show every extreme that they name: `lengths`: in every replica at least one utterance has all 128 frames.
All inputs are finite; a program needn't handle non-finite values.
Results may differ from a plain program's by a relative error of at most 0.004.
Values may be sent and summed in bfloat16 or wider, within the bound.
A program may use at most 128 MiB of HBM per device.

v0:
```python
import jax
import jax.numpy as jnp
from jax import lax
from jax.sharding import PartitionSpec as P

beta_one = 0.9
beta_two = 0.98
inner_rate = 0.08
decay_rate = 0.01
adam_eps = 1e-06
outer_rate = 0.7
nesterov_mu = 0.9
norm_eps = 1e-05
mix_weight = 0.5
inv_root_two = 0.7071067811865476
inv_root_tau = 0.3989422804014327
correction_one = 1.0 - beta_one**500.0
correction_two = 1.0 - beta_two**500.0


def gelu_parts(values):
    cumulative = 0.5 * (1.0 + jax.scipy.special.erf(values * inv_root_two))
    density = jnp.exp(-0.5 * values * values) * inv_root_tau
    return (values * cumulative, cumulative + values * density)


def normalize(mixed_rows):
    centre = jnp.mean(mixed_rows, axis=-1, keepdims=True)
    shifted = mixed_rows - centre
    spread = jnp.mean(shifted * shifted, axis=-1, keepdims=True)
    return (shifted * lax.rsqrt(spread + norm_eps)).astype(jnp.bfloat16)


def add_rows(left_rows, portion):
    return jnp.dot(left_rows, portion, preferred_element_type=jnp.float32)


def per_device(
    frames,
    cotangent,
    mix_partner,
    lengths,
    inner_params,
    first_moment,
    second_moment,
    outer_params,
    momentum,
):
    frame_rows = frames.shape[1]
    model_width = frames.shape[2]
    utt_count = mix_partner.shape[1]
    crop_frames = frame_rows // utt_count
    hidden_width = inner_params.shape[3]
    blocks = frames[0].reshape(utt_count, crop_frames, model_width).astype(jnp.float32)
    partner_rows = jnp.take(blocks, mix_partner[0], axis=0)
    mixed_rows = blocks + mix_weight * partner_rows
    normed = normalize(mixed_rows).reshape(frame_rows, model_width)
    offsets = lax.broadcasted_iota(jnp.int32, (utt_count, crop_frames), 1)
    keep_mask = (offsets < lengths[0][:, None]).reshape(frame_rows, 1).astype(jnp.bfloat16)
    masked_grad = cotangent[0] * keep_mask
    pre_sum = add_rows(normed, lax.all_gather(inner_params[0, :, 0, :], "fsdp", axis=0, tiled=True))
    back_sum = add_rows(
        masked_grad, lax.all_gather(inner_params[0, :, 1, :], "fsdp", axis=0, tiled=True)
    )
    pre_act = pre_sum * model_width ** (-0.5)
    back_grad = back_sum * hidden_width ** (-0.5)
    activation, derivative = gelu_parts(pre_act)
    activation = activation.astype(jnp.bfloat16)
    hidden_grad = (back_grad * derivative).astype(jnp.bfloat16)
    grad_in = lax.dot_general(
        normed, hidden_grad, (((0,), (0,)), ((), ())), preferred_element_type=jnp.float32
    ) * model_width ** (-0.5)
    grad_out = lax.dot_general(
        masked_grad, activation, (((0,), (0,)), ((), ())), preferred_element_type=jnp.float32
    ) * hidden_width ** (-0.5)
    gradients = lax.psum_scatter(
        jnp.stack((grad_in, grad_out), axis=1).astype(jnp.bfloat16),
        "fsdp",
        scatter_dimension=0,
        tiled=True,
    ).astype(jnp.float32)
    new_moment = beta_one * first_moment[0] + (1.0 - beta_one) * gradients
    new_second = beta_two * second_moment[0] + (1.0 - beta_two) * gradients * gradients
    update = new_moment / correction_one / (jnp.sqrt(new_second / correction_two) + adam_eps)
    current = inner_params[0].astype(jnp.float32)
    stepped = current - inner_rate * (update + decay_rate * current)
    pseudo = outer_params - stepped
    replica_count = lax.axis_size("group")
    totals = lax.psum(pseudo, "group")
    average = totals * (1.0 / replica_count)
    new_momentum = nesterov_mu * momentum + average
    new_outer = outer_params - outer_rate * (average + nesterov_mu * new_momentum)
    return (new_moment[None], new_outer, new_momentum)


def solution(mesh):
    in_specs = (
        P("group", "fsdp", None),
        P("group", "fsdp", None),
        P("group", "fsdp"),
        P("group", "fsdp"),
        P("group", "fsdp", None, None),
        P("group", "fsdp", None, None),
        P("group", "fsdp", None, None),
        P("fsdp", None, None),
        P("fsdp", None, None),
    )
    out_specs = (P("group", "fsdp", None, None), P("fsdp", None, None), P("fsdp", None, None))
    return jax.shard_map(
        per_device, mesh=mesh, in_specs=in_specs, out_specs=out_specs, check_vma=False
    )
```

profile of v0, /device:TPU:2, one launch (start us, length us, event | category | flops | bytes accessed | tf_op | source)
XLA Modules:
  0.0 577.6 jit_solution(5133253302970498098)
XLA Ops:
  7.2 0.0 copy-start
  7.2 0.0 all-gather.7.cloned.1.call-start
  7.2 2.9 fusion.36
  10.1 0.8 copy.50
  10.9 0.0 all-gather.7.cloned.1.call-update
  10.9 0.0 all-gather.5.cloned.1.call-start
  11.0 0.0 copy-start.7
  11.0 0.8 copy.51
  11.8 0.0 all-gather.5.cloned.1.call-update
  11.8 0.0 reduce-scatter.2.cloned.1.call-start
  11.9 0.0 copy-done
  11.9 1.7 convert.32
  13.6 0.0 copy-done.7
  13.6 0.0 copy-start.8
  13.6 2.5 gather_fusion
  16.1 0.0 copy-start.1
  16.1 0.1 broadcast_bitcast_fusion
  16.2 0.0 copy-done.8
  16.2 0.1 fusion.33
  16.2 2.0 fusion.28
  18.2 0.0 copy-done.1
  18.2 0.8 multiply_reduce_fusion
  19.0 1.7 fusion.16
  20.8 0.0 copy-start.6
  20.8 87.6 %all-gather.7.cloned.1.call-done = bf16[1,1280,1,2560]{3,1,2,0:T(8,128)(2,1)} async-done(((bf16[1,80,1,2560]{3,1,2,0:T(8,128)(2,1)}), bf16[1,1280,1,2560]{3,1,2,0:T(8,128)(2,1)}) %all-gather.7.cloned.1.call-update) | async-done | bytes 6553616 | tf_op jit(solution)/shard_map/all_gather | solution.py:61
  108.4 6.1 %fusion.4 = f32[512,2560]{1,0:T(8,128)S(1)} fusion(bf16[512,1280]{1,0:T(8,128)(2,1)} %fusion.16, bf16[1,1280,1,2560]{3,1,2,0:T(8,128)(2,1)} %all-gather.7.cloned.1.call-done), kind=kOutput, calls=%fused_computation.8 | convolution fusion | flops 3355443200 | bytes 13107200 | tf_op jit(solution)/shard_map/dot_general | solution.py:35
  114.4 0.0 copy-start.9
  114.4 2.3 copy-done.9
  116.7 0.0 copy-done.6
  116.7 5.8 %fusion.2 = bf16[1280,1,2560]{2,0,1:T(8,128)(2,1)} fusion(f32[512,2560]{1,0:T(8,128)S(1)} %fusion.4, bf16[1,512,1280]{2,1,0:T(8,128)(2,1)S(1)} %copy-done.6, bf16[512]{0:T(512)(128)(2,1)S(1)} %fusion.33), kind=kOutput, calls=%fused_computation.6 | convolution fusion | flops 3370516480 | bytes 13108224 | tf_op jit(solution)/shard_map/dot_general | solution.py:73
  122.5 0.0 copy-start.5
  122.5 79.0 %all-gather.5.cloned.1.call-done = bf16[1,1280,1,2560]{3,1,2,0:T(8,128)(2,1)} async-done(((bf16[1,80,1,2560]{3,1,2,0:T(8,128)(2,1)}), bf16[1,1280,1,2560]{3,1,2,0:T(8,128)(2,1)}) %all-gather.5.cloned.1.call-update) | async-done | bytes 6553616 | tf_op jit(solution)/shard_map/all_gather | solution.py:63
  201.6 7.9 %multiply_convert_fusion.1 = bf16[512,2560]{1,0:T(8,128)(2,1)S(1)} fusion(f32[512,2560]{1,0:T(8,128)} %copy-done.9, bf16[1,1280,1,2560]{3,1,2,0:T(8,128)(2,1)} %all-gather.5.cloned.1.call-done, bf16[1,512,1280]{2,1,0:T(8,128)(2,1)S(1)} %copy-done.6, bf16[512]{0:T(512)(128)(2,1)S(1)} %fusion.33), kind=kOutput, calls=%fused_computation.13 | convolution fusion | flops 3371827200 | bytes 15729664 | tf_op jit(solution)/shard_map/dot_general | solution.py:35
  209.5 0.0 copy-done.5
  209.5 0.0 copy-start.3
  209.5 3.9 fusion.3
  213.4 0.0 copy-done.3
  213.4 5.6 pad_maximum_fusion
  219.0 0.0 copy-start.2
  219.0 0.0 reduce-scatter.2.cloned.1.call-update
  219.0 0.2 all-reduce.2.cloned.1.call-start
  219.2 176.1 %reduce-scatter.2.cloned.1.call-done = bf16[80,2,2560]{2,0,1:T(8,128)(2,1)} async-done(((bf16[1280,2,2560]{2,0,1:T(8,128)(2,1)}), bf16[80,2,2560]{2,0,1:T(8,128)(2,1)}) %reduce-scatter.2.cloned.1.call-update) | async-done | bytes 819216 | tf_op jit(solution)/shard_map/reduce_scatter | solution.py:76
  395.3 0.0 copy-done.2
  395.3 5.4 fusion.21
  400.7 0.0 copy-start.4
  400.7 0.0 all-reduce.2.cloned.1.call-update
  400.8 2.4 copy.29
  403.2 160.2 %all-reduce.2.cloned.1.call-done = f32[80,2,2560]{2,0,1:T(8,128)} async-done(((f32[80,2,2560]{2,0,1:T(8,128)}), f32[80,2,2560]{2,0,1:T(8,128)}) %all-reduce.2.cloned.1.call-update) | async-done | bytes 1638416 | tf_op jit(solution)/shard_map/psum | solution.py:89
  563.4 0.0 copy-done.4
  563.4 2.8 fusion.27
  566.2 2.4 copy.31
  568.6 2.4 copy.30
  (5 shorter events, 0.0 us)
Async XLA Ops:
  7.2 4.7 copy-start
  7.2 101.2 %all-gather.7.cloned.1.call-start = ((), (), s32[]{:S(2)}) async-start(), calls=%async_computation.4 | async-start | bytes 6963200 | tf_op jit(solution)/shard_map/all_gather | solution.py:61
  10.9 190.6 %all-gather.5.cloned.1.call-start = ((), (), s32[]{:S(2)}) async-start(), calls=%async_computation.3 | async-start | bytes 6963200 | tf_op jit(solution)/shard_map/all_gather | solution.py:63
  11.0 2.6 copy-start.7
  11.8 383.5 %reduce-scatter.2.cloned.1.call-start = ((), (), s32[]{:S(2)}) async-start(), calls=%async_computation.1 | async-start | bytes 13926400 | tf_op jit(solution)/shard_map/reduce_scatter | solution.py:76
  13.6 2.6 copy-start.8
  16.1 2.2 copy-start.1
  20.8 96.0 %copy-start.6 = (bf16[1,512,1280]{2,1,0:T(8,128)(2,1)S(1)}, bf16[1,512,1280]{2,1,0:T(8,128)(2,1)}, u32[]{:S(2)}) copy-start(bf16[1,512,1280]{2,1,0:T(8,128)(2,1)} %param.10) | copy-start | bytes 3932164
  114.4 2.3 copy-start.9
  122.5 87.0 %copy-start.5 = (bf16[512,1280]{1,0:T(8,128)(2,1)S(1)}, bf16[512,1280]{1,0:T(8,128)(2,1)}, u32[]{:S(2)}) copy-start(bf16[512,1280]{1,0:T(8,128)(2,1)} %fusion.16) | copy-start | bytes 3932164
  209.5 3.9 copy-start.3
  219.0 176.4 %copy-start.2 = (bf16[1,80,2,2560]{3,2,1,0:T(2,128)(2,1)S(1)}, bf16[1,80,2,2560]{3,2,1,0:T(2,128)(2,1)}, u32[]{:S(2)}) copy-start(bf16[1,80,2,2560]{3,2,1,0:T(2,128)(2,1)} %param.13) | copy-start | bytes 2457604
  219.0 344.4 %all-reduce.2.cloned.1.call-start = ((), (), s32[]{:S(2)}) async-start(), calls=%async_computation.2 | async-start | bytes 3276800 | tf_op jit(solution)/shard_map/psum | solution.py:89
  400.7 162.7 %copy-start.4 = (f32[80,2,2560]{2,1,0:T(2,128)S(1)}, f32[80,2,2560]{2,1,0:T(2,128)}, u32[]{:S(2)}) copy-start(f32[80,2,2560]{2,1,0:T(2,128)} %param.16) | copy-start | bytes 4915204
Sparse Core Ops, SparseCore 0:
  11.3 97.0 all-gather.6
  111.6 89.9 all-gather.4
  219.1 176.1 reduce-scatter.1
  400.9 162.4 all-reduce.1
where the time goes:
time: 578 us
  waiting for transfers between devices  503 us (87%)
  matrix products  23.7 us (4%)
  other arithmetic  20 us (3%)
  local copies, waits for them, and re-layouts  16.6 us (3%)
  between operations  13.9 us (2%)
    reduce_scatter x1, waiting for transfers between devices, per_device(): lax.psum_scatter(jnp.stack((grad_in, grad_out), axis=1).astype(jnp.bfloat...  176 us
    psum x1, waiting for transfers between devices, per_device(): totals = lax.psum(pseudo, 'group')  160 us
    all_gather x1, waiting for transfers between devices, per_device(): lax.all_gather(inner_params[0, :, 0, :], 'fsdp', axis=0, tiled=True)  87.6 us
    all_gather x1, waiting for transfers between devices, per_device(): lax.all_gather(inner_params[0, :, 1, :], 'fsdp', axis=0, tiled=True)  79 us
    dot_general x2, matrix products, add_rows(): return jnp.dot(left_rows, portion, preferred_element_type=jnp.float32)  14 us
  transfers between devices with their start and end apart: 4, of which 4 were waited for; matrix products, arithmetic and copies ran while one was open for 4% of the time, Pallas kernels for 0%

commit v1 on v0

v1 whole, which is shorter than its diff:
```python
import jax
import jax.numpy as jnp
from jax import lax
from jax.sharding import Mesh, PartitionSpec as P

beta_one = 0.9
beta_two = 0.98
inner_rate = 0.08
decay_rate = 0.01
adam_eps = 1e-06
outer_rate = 0.7
nesterov_mu = 0.9
norm_eps = 1e-05
mix_weight = 0.5
inv_root_two = 0.7071067811865476
inv_root_tau = 0.3989422804014327
correction_one = 1.0 - beta_one**500.0
correction_two = 1.0 - beta_two**500.0

GROUP_PARTS = (("gz", 4), ("gy", 4))
FSDP_PARTS = (("fx", 4), ("fz", 2), ("fc", 2))
GROUP_AXES = tuple(name for name, _ in GROUP_PARTS)
FSDP_AXES = tuple(name for name, _ in FSDP_PARTS)
GATHER_ORDER = ("fz", "fx", "fc")


def gelu_parts(values):
    cumulative = 0.5 * (1.0 + jax.scipy.special.erf(values * inv_root_two))
    density = jnp.exp(-0.5 * values * values) * inv_root_tau
    return (values * cumulative, cumulative + values * density)


def normalize(mixed_rows):
    centre = jnp.mean(mixed_rows, axis=-1, keepdims=True)
    shifted = mixed_rows - centre
    spread = jnp.mean(shifted * shifted, axis=-1, keepdims=True)
    return (shifted * lax.rsqrt(spread + norm_eps)).astype(jnp.bfloat16)


def gathered_order(columns):
    sizes = dict(FSDP_PARTS)
    rows = columns.shape[0]
    local = columns.shape[1] // (sizes["fx"] * sizes["fz"] * sizes["fc"])
    split = columns.reshape(rows, sizes["fx"], sizes["fz"], sizes["fc"], local)
    position = {"fx": 1, "fz": 2, "fc": 3}
    order = (0,) + tuple(position[name] for name in reversed(GATHER_ORDER)) + (4,)
    return jnp.transpose(split, order).reshape(columns.shape)


def gather_rows(block):
    for name in GATHER_ORDER:
        block = lax.all_gather(block, name, axis=0, tiled=True)
    return block


def scatter_rows(block):
    for name in reversed(GATHER_ORDER):
        block = lax.psum_scatter(block, name, scatter_dimension=0, tiled=True)
    return block


def group_sum(values):
    shape = values.shape
    flat = values.reshape(-1, 128)
    for name in reversed(GROUP_AXES):
        flat = lax.psum_scatter(flat, name, scatter_dimension=0, tiled=True)
    for name in GROUP_AXES:
        flat = lax.all_gather(flat, name, axis=0, tiled=True)
    return flat.reshape(shape)


def per_device(
    frames,
    cotangent,
    mix_partner,
    lengths,
    inner_params,
    first_moment,
    second_moment,
    outer_params,
    momentum,
):
    frame_rows = frames.shape[1]
    model_width = frames.shape[2]
    utt_count = mix_partner.shape[1]
    crop_frames = frame_rows // utt_count
    hidden_width = inner_params.shape[3]
    blocks = frames[0].reshape(utt_count, crop_frames, model_width).astype(jnp.float32)
    partner_rows = jnp.take(blocks, mix_partner[0], axis=0)
    mixed_rows = blocks + mix_weight * partner_rows
    normed = normalize(mixed_rows).reshape(frame_rows, model_width)
    offsets = lax.broadcasted_iota(jnp.int32, (utt_count, crop_frames), 1)
    keep_mask = (offsets < lengths[0][:, None]).reshape(frame_rows, 1).astype(jnp.bfloat16)
    masked_grad = cotangent[0] * keep_mask
    normed = gathered_order(normed)
    masked_grad = gathered_order(masked_grad)

    w_in = gather_rows(inner_params[0, :, 0, :])
    pre_act = jnp.dot(normed, w_in, preferred_element_type=jnp.float32) * model_width ** (-0.5)
    cumulative = 0.5 * (1.0 + jax.scipy.special.erf(pre_act * inv_root_two))
    activation = (pre_act * cumulative).astype(jnp.bfloat16)
    grad_out = lax.dot_general(
        masked_grad, activation, (((0,), (0,)), ((), ())), preferred_element_type=jnp.float32
    ) * hidden_width ** (-0.5)
    grad_out = scatter_rows(grad_out.astype(jnp.bfloat16))

    w_out = gather_rows(inner_params[0, :, 1, :])
    back_grad = jnp.dot(masked_grad, w_out, preferred_element_type=jnp.float32) * hidden_width ** (-0.5)
    density = jnp.exp(-0.5 * pre_act * pre_act) * inv_root_tau
    hidden_grad = (back_grad * (cumulative + pre_act * density)).astype(jnp.bfloat16)
    grad_in = lax.dot_general(
        normed, hidden_grad, (((0,), (0,)), ((), ())), preferred_element_type=jnp.float32
    ) * model_width ** (-0.5)
    grad_in = scatter_rows(grad_in.astype(jnp.bfloat16))

    gradients = jnp.stack((grad_in, grad_out), axis=1).astype(jnp.float32)
    new_moment = beta_one * first_moment[0] + (1.0 - beta_one) * gradients
    new_second = beta_two * second_moment[0] + (1.0 - beta_two) * gradients * gradients
    update = new_moment / correction_one / (jnp.sqrt(new_second / correction_two) + adam_eps)
    current = inner_params[0].astype(jnp.float32)
    stepped = current - inner_rate * (update + decay_rate * current)
    pseudo = outer_params - stepped
    replica_count = 1
    for _, size in GROUP_PARTS:
        replica_count *= size
    totals = group_sum(pseudo)
    average = totals * (1.0 / replica_count)
    new_momentum = nesterov_mu * momentum + average
    new_outer = outer_params - outer_rate * (average + nesterov_mu * new_momentum)
    return (new_moment[None], new_outer, new_momentum)


def solution(mesh):
    sizes = tuple(size for _, size in GROUP_PARTS + FSDP_PARTS)
    split_mesh = Mesh(mesh.devices.reshape(sizes), GROUP_AXES + FSDP_AXES)
    group, fsdp = GROUP_AXES, FSDP_AXES
    in_specs = (
        P(group, fsdp, None),
        P(group, fsdp, None),
        P(group, fsdp),
        P(group, fsdp),
        P(group, fsdp, None, None),
        P(group, fsdp, None, None),
        P(group, fsdp, None, None),
        P(fsdp, None, None),
        P(fsdp, None, None),
    )
    out_specs = (P(group, fsdp, None, None), P(fsdp, None, None), P(fsdp, None, None))
    return jax.shard_map(
        per_device, mesh=split_mesh, in_specs=in_specs, out_specs=out_specs, check_vma=False
    )
```

time: 578 us -> 520 us (0.90)
  the two profiles are of different devices: /device:TPU:2 before, /device:TPU:121 now
where the time goes in v1:
time: 520 us; the launch traced here: 516 us
  waiting for transfers between devices  370 us (71%)
  blocking collectives  50.9 us (10%)
  local copies, waits for them, and re-layouts  33.8 us (6%)
  matrix products  29.7 us (6%)
  other arithmetic  16.3 us (3%)
  between operations  14.1 us (3%)
    reduce_scatter x6, waiting for transfers between devices, scatter_rows(): block = lax.psum_scatter(block, name, scatter_dimension=0, tiled=True)  197 us
    all_gather x4, waiting for transfers between devices, gather_rows(): block = lax.all_gather(block, name, axis=0, tiled=True)  90.7 us
    all_gather x2, blocking collectives, gather_rows(): block = lax.all_gather(block, name, axis=0, tiled=True)  36 us
    all_gather x1, waiting for transfers between devices, group_sum(): flat = lax.all_gather(flat, name, axis=0, tiled=True)  30.5 us
    reduce_scatter x1, waiting for transfers between devices, group_sum(): flat = lax.psum_scatter(flat, name, scatter_dimension=0, tiled=True)  26.2 us
    unnamed x14, waiting for transfers between devices  25.6 us
    gather x4, local copies, waits for them, and re-layouts, per_device(): partner_rows = jnp.take(blocks, mix_partner[0], axis=0)  16.2 us
    all_gather x1, blocking collectives, group_sum(): flat = lax.all_gather(flat, name, axis=0, tiled=True)  15 us
  transfers between devices with their start and end apart: 13, of which 12 were waited for; matrix products, arithmetic and copies ran while one was open for 9% of the time, Pallas kernels for 0%

profile of v1, /device:TPU:121, one launch (start us, length us, event | category | flops | bytes accessed | tf_op | source)
XLA Modules:
  0.0 515.9 jit_solution(13099699792472657934)
XLA Ops:
  7.2 0.0 all-gather.18.cloned.1.call-start
  7.2 2.8 fusion.24
  10.0 0.1 copy.69
  10.1 19.0 %all-gather.3 = bf16[1,160,1,2560]{3,1,2,0:T(8,128)(2,1)} all-gather(bf16[1,80,1,2560]{3,1,2,0:T(8,128)(2,1)S(1)} %copy.69), channel_id=5, replica_groups=mesh['gz'=4,'gy'=4,'fx'=4,'fz'=2,'fc'=2] {'fz'}, dimensions={1}, use_global_device_ids=true | all-gather | bytes 1228800 | tf_op jit(solution)/shard_map/all_gather | solution.py:52
  29.1 0.0 all-gather.14.cloned.1.call-start
  29.2 0.1 copy.70
  29.3 16.9 %all-gather = bf16[1,160,1,2560]{3,1,2,0:T(8,128)(2,1)} all-gather(bf16[1,80,1,2560]{3,1,2,0:T(8,128)(2,1)S(1)} %copy.70), channel_id=2, replica_groups=mesh['gz'=4,'gy'=4,'fx'=4,'fz'=2,'fc'=2] {'fz'}, dimensions={1}, use_global_device_ids=true | all-gather | bytes 1228800 | tf_op jit(solution)/shard_map/all_gather | solution.py:52
  46.2 0.0 all-gather.20.cloned.1.call-start
  46.2 33.1 %all-gather.18.cloned.1.call-done = bf16[1,640,1,2560]{3,1,2,0:T(8,128)(2,1)} async-done(((bf16[1,160,1,2560]{3,1,2,0:T(8,128)(2,1)}), bf16[1,640,1,2560]{3,1,2,0:T(8,128)(2,1)}) %all-gather.18.cloned.1.call-update) | async-done | bytes 3276816 | tf_op jit(solution)/shard_map/all_gather | solution.py:52
  79.3 0.0 all-gather.16.cloned.1.call-start
  79.4 45.2 %all-gather.14.cloned.1.call-done = bf16[1,640,1,2560]{3,1,2,0:T(8,128)(2,1)} async-done(((bf16[1,160,1,2560]{3,1,2,0:T(8,128)(2,1)}), bf16[1,640,1,2560]{3,1,2,0:T(8,128)(2,1)}) %all-gather.14.cloned.1.call-update) | async-done | bytes 3276816 | tf_op jit(solution)/shard_map/all_gather | solution.py:52
  124.6 0.0 reduce-scatter.12.cloned.1.call-start
  124.7 0.7 copy.45
  125.3 1.9 copy.46
  127.2 1.9 convert_element_type.77
  129.2 4.0 gather_fusion
  133.1 4.1 copy.47
  137.3 3.6 copy.48
  140.9 4.5 gather.9
  145.4 0.1 broadcast_bitcast_fusion
  145.5 2.4 fusion.19
  147.9 0.2 copy-done
  148.0 0.6 multiply_reduce_fusion
  148.7 0.1 copy-done.2
  148.8 1.0 copy-done.1
  149.8 0.7 fusion.18
  150.6 1.1 copy.49
  151.8 0.6 copy-done.8
  152.4 0.6 copy.50
  153.0 0.1 fusion.21
  153.1 0.1 multiply_bitcast_fusion
  153.2 0.1 copy.51
  153.3 1.1 copy-done.9
  154.4 8.2 %fusion.2 = f32[512,2560]{1,0:T(8,128)} fusion(bf16[512,1280]{0,1:T(8,128)(2,1)S(1)} %bitcast.58, bf16[1,1280,1,2560]{3,1,2,0:T(8,128)(2,1)} %all-gather.20.cloned.1.call-done), kind=kOutput, calls=%fused_computation.5 | convolution fusion | flops 3355443200 | bytes 13107200 | tf_op jit(solution)/shard_map/dot_general | solution.py:99
  162.6 12.5 %all-gather.16.cloned.1.call-done = bf16[1,1280,1,2560]{3,1,2,0:T(8,128)(2,1)} async-done(((bf16[1,640,1,2560]{3,1,2,0:T(8,128)(2,1)}), bf16[1,1280,1,2560]{3,1,2,0:T(8,128)(2,1)}) %all-gather.16.cloned.1.call-update) | async-done | bytes 6553616 | tf_op jit(solution)/shard_map/all_gather | solution.py:52
  175.1 8.5 %multiply_convert_fusion.1 = bf16[512,2560]{1,0:T(8,128)(2,1)S(1)} fusion(f32[512,2560]{1,0:T(8,128)} %fusion.2, bf16[512,1280]{0,1:T(8,128)(2,1)S(1)} %bitcast.56, bf16[1,1280,1,2560]{3,1,2,0:T(8,128)(2,1)} %all-gather.16.cloned.1.call-done), kind=kOutput, calls=%fused_computation.10 | convolution fusion | flops 3371171840 | bytes 15728640 | tf_op jit(solution)/shard_map/dot_general | solution.py:108
  183.6 5.5 %fusion = bf16[1280,2560]{1,0:T(8,128)(2,1)} fusion(bf16[512,1280]{0,1:T(8,128)(2,1)S(1)} %bitcast.59, bf16[512,2560]{1,0:T(8,128)(2,1)S(1)} %multiply_convert_fusion.1), kind=kOutput, calls=%fused_computation.3 | convolution fusion | flops 3361996800 | bytes 10485760 | tf_op jit(solution)/shard_map/dot_general | solution.py:111
  189.2 0.2 reduce-scatter.18.cloned.1.call-start
  189.4 7.4 %fusion.1 = bf16[1280,2560]{1,0:T(8,128)(2,1)} fusion(bf16[512,1280]{0,1:T(8,128)(2,1)S(1)} %bitcast.57, f32[512,2560]{1,0:T(8,128)} %fusion.2), kind=kOutput, calls=%fused_computation.4 | convolution fusion | flops 3369861120 | bytes 13107200 | tf_op jit(solution)/shard_map/dot_general | solution.py:102
  196.8 0.0 reduce-scatter.14.cloned.1.call-start
  196.9 13.9 %reduce-scatter.12.cloned.1.call-done = bf16[640,2560]{1,0:T(8,128)(2,1)} async-done(((bf16[1280,2560]{1,0:T(8,128)(2,1)}), bf16[640,2560]{1,0:T(8,128)(2,1)}) %reduce-scatter.12.cloned.1.call-update) | async-done | bytes 3276816 | tf_op jit(solution)/shard_map/reduce_scatter | solution.py:58
  210.8 0.0 reduce-scatter.20.cloned.1.call-start
  210.8 24.0 %reduce-scatter.18.cloned.1.call-done = bf16[640,2560]{1,0:T(8,128)(2,1)} async-done(((bf16[1280,2560]{1,0:T(8,128)(2,1)}), bf16[640,2560]{1,0:T(8,128)(2,1)}) %reduce-scatter.18.cloned.1.call-update) | async-done | bytes 3276816 | tf_op jit(solution)/shard_map/reduce_scatter | solution.py:58
  234.8 0.0 reduce-scatter.16.cloned.1.call-start
  234.9 45.2 %reduce-scatter.14.cloned.1.call-done = bf16[160,2560]{1,0:T(8,128)(2,1)} async-done(((bf16[640,2560]{1,0:T(8,128)(2,1)}), bf16[160,2560]{1,0:T(8,128)(2,1)}) %reduce-scatter.14.cloned.1.call-update) | async-done | bytes 819216 | tf_op jit(solution)/shard_map/reduce_scatter | solution.py:58
  280.1 0.0 reduce-scatter.22.cloned.1.call-start
  280.2 44.1 %reduce-scatter.20.cloned.1.call-done = bf16[160,2560]{1,0:T(8,128)(2,1)} async-done(((bf16[640,2560]{1,0:T(8,128)(2,1)}), bf16[160,2560]{1,0:T(8,128)(2,1)}) %reduce-scatter.20.cloned.1.call-update) | async-done | bytes 819216 | tf_op jit(solution)/shard_map/reduce_scatter | solution.py:58
  324.3 0.0 reduce-scatter.24.cloned.1.call-start
  324.4 35.5 %reduce-scatter.16.cloned.1.call-done = bf16[80,2560]{1,0:T(8,128)(2,1)} async-done(((bf16[160,2560]{1,0:T(8,128)(2,1)}), bf16[80,2560]{1,0:T(8,128)(2,1)}) %reduce-scatter.16.cloned.1.call-update) | async-done | bytes 409616 | tf_op jit(solution)/shard_map/reduce_scatter | solution.py:58
  359.9 34.7 %reduce-scatter.22.cloned.1.call-done = bf16[80,2560]{1,0:T(8,128)(2,1)} async-done(((bf16[160,2560]{1,0:T(8,128)(2,1)}), bf16[80,2560]{1,0:T(8,128)(2,1)}) %reduce-scatter.22.cloned.1.call-update) | async-done | bytes 409616 | tf_op jit(solution)/shard_map/reduce_scatter | solution.py:58
  394.6 3.7 fusion.13
  398.2 1.3 copy.57
  399.5 2.5 reshape.188
  402.0 0.0 reduce-scatter.26.cloned.1.call-start
  402.1 26.2 %reduce-scatter.24.cloned.1.call-done = f32[800,128]{1,0:T(8,128)} async-done(((f32[3200,128]{1,0:T(8,128)}), f32[800,128]{1,0:T(8,128)}) %reduce-scatter.24.cloned.1.call-update) | async-done | bytes 409616 | tf_op jit(solution)/shard_map/reduce_scatter | solution.py:66
  428.3 0.0 all-gather.12.cloned.1.call-start
  428.3 25.4 %reduce-scatter.26.cloned.1.call-done = f32[200,128]{1,0:T(8,128)} async-done(((f32[800,128]{1,0:T(8,128)}), f32[200,128]{1,0:T(8,128)}) %reduce-scatter.26.cloned.1.call-update) | async-done | bytes 102416
  453.7 15.0 %all_gather.30 = f32[800,128]{1,0:T(8,128)} all-gather(f32[200,128]{1,0:T(8,128)} %reduce-scatter.26.cloned.1.call-done), channel_id=1, replica_groups=mesh['gz'=4,'gy'=4,'fx'=4,'fz'=2,'fc'=2] {'gz'}, dimensions={0}, use_global_device_ids=true | all-gather | bytes 512000 | tf_op jit(solution)/shard_map/all_gather | solution.py:68
  468.8 0.4 multiply_add_fusion.2
  469.2 2.4 copy.58
  471.6 30.5 %all-gather.12.cloned.1.call-done = f32[3200,128]{1,0:T(8,128)} async-done(((f32[800,128]{1,0:T(8,128)}), f32[3200,128]{1,0:T(8,128)}) %all-gather.12.cloned.1.call-update) | async-done | bytes 1638416 | tf_op jit(solution)/shard_map/all_gather | solution.py:68
  502.1 1.5 broadcast_multiply_fusion
  503.7 0.9 mul.220
  504.5 4.8 multiply_subtract_fusion
  (38 shorter events, 0.3 us)
Async XLA Ops:
  7.2 72.2 %all-gather.18.cloned.1.call-start = ((), (), s32[]{:S(2)}) async-start(), calls=%async_computation.18 | async-start | bytes 4096000 | tf_op jit(solution)/shard_map/all_gather | solution.py:52
  29.1 95.4 %all-gather.14.cloned.1.call-start = ((), (), s32[]{:S(2)}) async-start(), calls=%async_computation.16 | async-start | bytes 4096000 | tf_op jit(solution)/shard_map/all_gather | solution.py:52
  46.2 107.1 %all-gather.20.cloned.1.call-start = ((), (), s32[]{:S(2)}) async-start(), calls=%async_computation.19 | async-start | bytes 9830400 | tf_op jit(solution)/shard_map/all_gather | solution.py:52
  79.3 45.3 %copy-start.7 = (bf16[1,512,1280]{2,1,0:T(8,128)(2,1)S(1)}, bf16[1,512,1280]{2,1,0:T(8,128)(2,1)}, u32[]{:S(2)}) copy-start(bf16[1,512,1280]{2,1,0:T(8,128)(2,1)} %param.9) | copy-start | bytes 3932164
  79.3 95.7 %all-gather.16.cloned.1.call-start = ((), (), s32[]{:S(2)}) async-start(), calls=%async_computation.17 | async-start | bytes 9830400 | tf_op jit(solution)/shard_map/all_gather | solution.py:52
  124.6 86.2 %reduce-scatter.12.cloned.1.call-start = ((), (), s32[]{:S(2)}) async-start(), calls=%async_computation.8 | async-start | bytes 9830400 | tf_op jit(solution)/shard_map/reduce_scatter | solution.py:58
  127.2 1.9 copy-start.10
  145.4 2.7 copy-start
  145.5 3.4 copy-start.2
  147.9 2.0 copy-start.1
  150.6 1.8 copy-start.8
  150.6 2.4 copy-start.11
  153.1 1.3 copy-start.9
  189.2 45.6 %reduce-scatter.18.cloned.1.call-start = ((), (), s32[]{:S(2)}) async-start(), calls=%async_computation.11 | async-start | bytes 9830400 | tf_op jit(solution)/shard_map/reduce_scatter | solution.py:58
  196.8 83.3 %reduce-scatter.14.cloned.1.call-start = ((), (), s32[]{:S(2)}) async-start(), calls=%async_computation.9 | async-start | bytes 4096000 | tf_op jit(solution)/shard_map/reduce_scatter | solution.py:58
  210.8 183.8 %copy-start.3 = (bf16[1,80,2,2560]{3,2,1,0:T(2,128)(2,1)S(1)}, bf16[1,80,2,2560]{3,2,1,0:T(2,128)(2,1)}, u32[]{:S(2)}) copy-start(bf16[1,80,2,2560]{3,2,1,0:T(2,128)(2,1)} %param.13) | copy-start | bytes 2457604
  210.8 183.8 %copy-start.4 = (f32[1,80,2,2560]{3,2,1,0:T(2,128)S(1)}, f32[1,80,2,2560]{3,2,1,0:T(2,128)}, u32[]{:S(2)}) copy-start(f32[1,80,2,2560]{3,2,1,0:T(2,128)} %param.14) | copy-start | bytes 4915204
  210.8 113.5 %reduce-scatter.20.cloned.1.call-start = ((), (), s32[]{:S(2)}) async-start(), calls=%async_computation.12 | async-start | bytes 4096000 | tf_op jit(solution)/shard_map/reduce_scatter | solution.py:58
  234.8 125.0 %reduce-scatter.16.cloned.1.call-start = ((), (), s32[]{:S(2)}) async-start(), calls=%async_computation.10 | async-start | bytes 1228800 | tf_op jit(solution)/shard_map/reduce_scatter | solution.py:58
  280.1 114.4 %reduce-scatter.22.cloned.1.call-start = ((), (), s32[]{:S(2)}) async-start(), calls=%async_computation.13 | async-start | bytes 1228800 | tf_op jit(solution)/shard_map/reduce_scatter | solution.py:58
  324.3 103.9 %reduce-scatter.24.cloned.1.call-start = ((), (), s32[]{:S(2)}) async-start(), calls=%async_computation.14 | async-start | bytes 2048000 | tf_op jit(solution)/shard_map/reduce_scatter | solution.py:66
  402.0 66.8 %copy-start.5 = (bf16[80,2560]{1,0:T(8,128)(2,1)S(1)}, bf16[80,2560]{1,0:T(8,128)(2,1)}, u32[]{:S(2)}) copy-start(bf16[80,2560]{1,0:T(8,128)(2,1)} %reduce-scatter.16.cloned.1.call-done) | copy-start | bytes 1228804
  402.0 66.8 %copy-start.6 = (bf16[80,2560]{1,0:T(8,128)(2,1)S(1)}, bf16[80,2560]{1,0:T(8,128)(2,1)}, u32[]{:S(2)}) copy-start(bf16[80,2560]{1,0:T(8,128)(2,1)} %reduce-scatter.22.cloned.1.call-done) | copy-start | bytes 1228804
  402.0 51.7 %reduce-scatter.26.cloned.1.call-start = ((), (), s32[]{:S(2)}) async-start(), calls=%async_computation.20 | async-start | bytes 512000
  428.3 73.8 %all-gather.12.cloned.1.call-start = ((), (), s32[]{:S(2)}) async-start(), calls=%async_computation.15 | async-start | bytes 2048000 | tf_op jit(solution)/shard_map/all_gather | solution.py:68
Sparse Core Ops, SparseCore 0:
  29.3 50.0 all-gather.17
  81.1 43.3 all-gather.13
  126.4 23.1 all-gather.19
  151.2 23.7 all-gather.15
  189.3 21.4 reduce-scatter.11
  213.3 21.4 reduce-scatter.17
  237.4 42.7 reduce-scatter.13
  282.7 41.5 reduce-scatter.19
  326.8 32.9 reduce-scatter.15
  362.2 32.3 reduce-scatter.21
  402.1 26.0 reduce-scatter.23
  430.8 22.8 reduce-scatter.25
  468.9 33.1 all-gather.11

commit v2 on v1

--- a/solution.py
+++ b/solution.py
@@ -21,7 +21,6 @@
 FSDP_PARTS = (("fx", 4), ("fz", 2), ("fc", 2))
 GROUP_AXES = tuple(name for name, _ in GROUP_PARTS)
 FSDP_AXES = tuple(name for name, _ in FSDP_PARTS)
-GATHER_ORDER = ("fz", "fx", "fc")
 
 
 def gelu_parts(values):
@@ -42,21 +41,27 @@
     rows = columns.shape[0]
     local = columns.shape[1] // (sizes["fx"] * sizes["fz"] * sizes["fc"])
     split = columns.reshape(rows, sizes["fx"], sizes["fz"], sizes["fc"], local)
-    position = {"fx": 1, "fz": 2, "fc": 3}
-    order = (0,) + tuple(position[name] for name in reversed(GATHER_ORDER)) + (4,)
-    return jnp.transpose(split, order).reshape(columns.shape)
+    split = jnp.where(lax.axis_index("fz") == 0, split, jnp.flip(split, axis=2))
+    split = jnp.where(lax.axis_index("fc") == 0, split, jnp.flip(split, axis=3))
+    return jnp.transpose(split, (0, 3, 1, 2, 4)).reshape(columns.shape)
+
+
+def swap(block, name):
+    return lax.ppermute(block, name, perm=[(0, 1), (1, 0)])
 
 
 def gather_rows(block):
-    for name in GATHER_ORDER:
-        block = lax.all_gather(block, name, axis=0, tiled=True)
-    return block
+    block = jnp.concatenate([block, swap(block, "fz")], axis=0)
+    block = lax.all_gather(block, "fx", axis=0, tiled=True)
+    return jnp.concatenate([block, swap(block, "fc")], axis=0)
 
 
 def scatter_rows(block):
-    for name in reversed(GATHER_ORDER):
-        block = lax.psum_scatter(block, name, scatter_dimension=0, tiled=True)
-    return block
+    half = block.shape[0] // 2
+    block = block[:half].astype(jnp.float32) + swap(block[half:], "fc").astype(jnp.float32)
+    block = lax.psum_scatter(block.astype(jnp.bfloat16), "fx", scatter_dimension=0, tiled=True)
+    half = block.shape[0] // 2
+    return block[:half].astype(jnp.float32) + swap(block[half:], "fz").astype(jnp.float32)
 
 
 def group_sum(values):

time: 520 us -> 409 us (0.79)
  waiting for transfers between devices: 370 us -> 270 us
  blocking collectives: 50.9 us -> 15.9 us
  starting transfers between devices: 0.69 us -> 18.3 us
  other arithmetic: 16.3 us -> 28.4 us
  matrix products: 29.7 us -> 22.2 us
    reduce_scatter x6 -> x2, waiting for transfers between devices: 197 us -> 67.2 us  [scatter_rows(): lax.psum_scatter(block.astype(jnp.bfloat16), 'fx', scatter_dimension=0, t...]
    ppermute x0 -> x8, waiting for transfers between devices: none -> 49.4 us  [swap(): return lax.ppermute(block, name, perm=[(0, 1), (1, 0)])]
    all_gather x2 -> x0, blocking collectives: 36 us -> none  [gather_rows(): block = lax.all_gather(block, name, axis=0, tiled=True)]
    all_gather x4 -> x2, waiting for transfers between devices: 90.7 us -> 66.1 us  [gather_rows(): block = lax.all_gather(block, 'fx', axis=0, tiled=True)]
    ppermute x0 -> x8, starting transfers between devices: none -> 17.8 us  [swap(): return lax.ppermute(block, name, perm=[(0, 1), (1, 0)])]
    convert_element_type x0 -> x3, other arithmetic: none -> 5.91 us  [the longest x2 5.17 us: scatter_rows(): block.astype(jnp.bfloat16)]
    reduce_scatter x1, waiting for transfers between devices: 26.2 us -> 31.8 us  [group_sum(): flat = lax.psum_scatter(flat, name, scatter_dimension=0, tiled=True)]
    unnamed x29 -> x32, local copies, waits for them, and re-layouts: 6.92 us -> 10.5 us
  transfers between devices with their start and end apart: 13 -> 15, of which waited for: 12 -> 12; matrix products, arithmetic and copies ran while one was open for 9% -> 13% of each run, Pallas kernels for 0% -> 0%
where the time goes in v2:
time: 409 us; the launch traced here: 405 us
  waiting for transfers between devices  270 us (66%)
  local copies, waits for them, and re-layouts  35.6 us (9%)
  other arithmetic  28.4 us (7%)
  matrix products  22.2 us (5%)
  starting transfers between devices  18.3 us (4%)
  blocking collectives  15.9 us (4%)
  between operations  14.5 us (4%)
    reduce_scatter x2, waiting for transfers between devices, scatter_rows(): lax.psum_scatter(block.astype(jnp.bfloat16), 'fx', scatter_dimension=0, t...  67.2 us
    all_gather x2, waiting for transfers between devices, gather_rows(): block = lax.all_gather(block, 'fx', axis=0, tiled=True)  66.1 us
    ppermute x8, waiting for transfers between devices, swap(): return lax.ppermute(block, name, perm=[(0, 1), (1, 0)])  49.4 us
    reduce_scatter x1, waiting for transfers between devices, group_sum(): flat = lax.psum_scatter(flat, name, scatter_dimension=0, tiled=True)  31.8 us
    all_gather x1, waiting for transfers between devices, group_sum(): flat = lax.all_gather(flat, name, axis=0, tiled=True)  29.9 us
    unnamed x8, waiting for transfers between devices  25.4 us
    ppermute x8, starting transfers between devices, swap(): return lax.ppermute(block, name, perm=[(0, 1), (1, 0)])  17.8 us
    all_gather x1, blocking collectives, group_sum(): flat = lax.all_gather(flat, name, axis=0, tiled=True)  15.9 us
  transfers between devices with their start and end apart: 15, of which 12 were waited for; matrix products, arithmetic and copies ran while one was open for 13% of the time, Pallas kernels for 0%

profile of v2, /device:TPU:121, one launch (start us, length us, event | category | flops | bytes accessed | tf_op | source)
XLA Modules:
  0.0 404.8 jit_solution(14957014470577986936)
XLA Ops:
  7.2 1.2 copy.52
  8.5 4.3 %collective-permute-start.2 = (bf16[80,2560]{1,0:T(8,128)(2,1)S(1)}, bf16[80,2560]{1,0:T(8,128)(2,1)S(1)}, u32[]{:S(2)}, u32[]{:S(2)}) collective-permute-start(bf16[80,2560]{1,0:T(8,128)(2,1)S(1)} %get-tuple-element.22), channel_id=1, source_target_pairs={{0,2},{2,0},{1,3},{3,1},{4,6},{6,4},{5,7},{7,5},{8,10},{10,8},{9,1... | collective-permute-start | bytes 1228808 | tf_op jit(solution)/shard_map/ppermute | solution.py:50
  12.8 14.2 %collective-permute-done.2 = bf16[80,2560]{1,0:T(8,128)(2,1)S(1)} collective-permute-done((bf16[80,2560]{1,0:T(8,128)(2,1)S(1)}, bf16[80,2560]{1,0:T(8,128)(2,1)S(1)}, u32[]{:S(2)}, u32[]{:S(2)}) %collective-permute-start.2) | collective-permute-done | bytes 409632 | tf_op jit(solution)/shard_map/ppermute | solution.py:50
  27.0 0.9 pad_maximum_fusion.2
  28.0 6.2 %collective-permute-start = (bf16[80,2560]{1,0:T(8,128)(2,1)S(1)}, bf16[80,2560]{1,0:T(8,128)(2,1)S(1)}, u32[]{:S(2)}, u32[]{:S(2)}) collective-permute-start(bf16[80,2560]{1,0:T(8,128)(2,1)S(1)} %get-tuple-element.21), channel_id=1, source_target_pairs={{0,2},{2,0},{1,3},{3,1},{4,6},{6,4},{5,7},{7,5},{8,10},{10,8},{9,1... | collective-permute-start | bytes 1228808 | tf_op jit(solution)/shard_map/ppermute | solution.py:50
  34.2 9.6 %collective-permute-done = bf16[80,2560]{1,0:T(8,128)(2,1)S(1)} collective-permute-done((bf16[80,2560]{1,0:T(8,128)(2,1)S(1)}, bf16[80,2560]{1,0:T(8,128)(2,1)S(1)}, u32[]{:S(2)}, u32[]{:S(2)}) %collective-permute-start) | collective-permute-done | bytes 409632 | tf_op jit(solution)/shard_map/ppermute | solution.py:50
  43.7 0.9 pad_maximum_fusion.1
  44.8 0.7 copy.45
  45.4 1.9 copy.46
  47.4 4.1 %gather_fusion = f32[4,128,1280]{2,1,0:T(8,128)} fusion(f32[4,128,1280]{2,1,0:T(8,128)} %bitcast.52, s32[1024]{0:T(1024)S(1)} %pad_clamp_fusion), kind=kCustom, calls=%fused_computation | custom fusion | bytes 5242896 | tf_op jit(solution)/shard_map/jit(_take)/gather | solution.py:94
  51.5 3.3 copy.48
  54.8 23.2 %all-gather.6.cloned.1.call-done = bf16[640,2560]{1,0:T(8,128)(2,1)} async-done(((bf16[160,2560]{1,0:T(8,128)(2,1)}), bf16[640,2560]{1,0:T(8,128)(2,1)}) %all-gather.6.cloned.1.call-update) | async-done | bytes 3276816 | tf_op jit(solution)/shard_map/all_gather | solution.py:55
  78.0 0.7 collective-permute-start.3
  78.7 2.2 fusion.24
  81.0 42.8 %all-gather.4.cloned.1.call-done = bf16[640,2560]{1,0:T(8,128)(2,1)} async-done(((bf16[160,2560]{1,0:T(8,128)(2,1)}), bf16[640,2560]{1,0:T(8,128)(2,1)}) %all-gather.4.cloned.1.call-update) | async-done | bytes 3276816 | tf_op jit(solution)/shard_map/all_gather | solution.py:55
  123.8 0.7 collective-permute-start.1
  124.6 4.1 %copy.47 = f32[4,128,1280]{1,0,2:T(4,128)} copy(f32[4,128,1280]{2,1,0:T(8,128)} %gather_fusion) | data formatting | bytes 5242880 | tf_op jit(solution)/shard_map/jit(_take)/gather | solution.py:94
  128.7 1.9 convert_element_type.103
  130.6 4.1 %gather.9 = f32[512,4,2,2,80]{0,4,3,2,1:T(8,128)} reshape(f32[4,128,1280]{1,0,2:T(4,128)} %copy.47) | data formatting | bytes 5242880 | tf_op jit(solution)/shard_map/jit(_take)/gather | solution.py:94
  134.7 1.6 copy.50
  136.3 2.5 multiply_reduce_fusion
  138.9 0.1 broadcast_multiply_fusion.1
  139.0 0.7 copy-done.1
  139.6 0.7 multiply_convert_fusion.3
  140.4 0.7 reverse_select_fusion.1
  141.1 0.3 fusion.22
  141.4 0.1 copy.49
  141.5 0.3 fusion.23
  141.9 1.5 copy-done.9
  143.4 5.5 %fusion.6 = f32[512,2560]{1,0:T(8,128)S(1)} fusion(bf16[512,1280]{0,1:T(8,128)(2,1)S(1)} %bitcast.56, bf16[640,2560]{1,0:T(8,128)(2,1)} %collective-permute-done.3, bf16[640,2560]{1,0:T(8,128)(2,1)S(1)} %copy-done.9), kind=kOutput, calls=%fused_computation.9 | convolution fusion | flops 3368550400 | bytes 13107200 | tf_op jit(solution)/shard_map/dot_general | solution.py:104
  148.9 2.4 copy-done.13
  151.3 7.3 %multiply_convert_fusion.1 = bf16[512,2560]{1,0:T(8,128)(2,1)S(1)} fusion(f32[512,2560]{1,0:T(8,128)S(1)} %fusion.6, bf16[512,1280]{0,1:T(8,128)(2,1)S(1)} %bitcast.54, bf16[640,2560]{1,0:T(8,128)(2,1)} %collective-permute-done.1, bf16[640,2560]{1,0:T(8,128)(2,1)S(1)} %copy-done.10), kind=kOutput, calls=%fused_computation.16 | convolution fusion | flops 3384279040 | bytes 15728640 | tf_op jit(solution)/shard_map/dot_general | solution.py:113
  158.5 3.8 fusion
  162.3 0.2 slice.45
  162.6 0.1 collective-permute-start.4
  162.7 5.8 %collective-permute-done.4 = bf16[640,2560]{1,0:T(8,128)(2,1)S(1)} collective-permute-done((bf16[640,2560]{1,0:T(8,128)(2,1)S(1)}, bf16[640,2560]{1,0:T(8,128)(2,1)S(1)}, u32[]{:S(2)}, u32[]{:S(2)}) %collective-permute-start.4) | collective-permute-done | bytes 3276832 | tf_op jit(solution)/shard_map/ppermute | solution.py:50
  168.5 2.6 add_convert_fusion.1
  171.1 0.3 reduce-scatter.10.cloned.1.call-start
  171.4 5.7 %fusion.1 = bf16[1280,2560]{1,0:T(8,128)(2,1)S(1)} fusion(bf16[512,1280]{0,1:T(8,128)(2,1)S(1)} %bitcast.55, f32[512,2560]{1,0:T(8,128)} %copy-done.13), kind=kOutput, calls=%fused_computation.4 | convolution fusion | flops 3369861120 | bytes 13107200 | tf_op jit(solution)/shard_map/dot_general | solution.py:107
  177.1 0.2 slice.49
  177.3 0.2 collective-permute-start.6
  177.5 5.7 %collective-permute-done.6 = bf16[640,2560]{1,0:T(8,128)(2,1)S(1)} collective-permute-done((bf16[640,2560]{1,0:T(8,128)(2,1)S(1)}, bf16[640,2560]{1,0:T(8,128)(2,1)S(1)}, u32[]{:S(2)}, u32[]{:S(2)}) %collective-permute-start.6) | collective-permute-done | bytes 3276832 | tf_op jit(solution)/shard_map/ppermute | solution.py:50
  183.2 2.6 add_convert_fusion
  185.9 27.0 %reduce-scatter.8.cloned.1.call-done = bf16[160,2560]{1,0:T(8,128)(2,1)} async-done(((bf16[640,2560]{1,0:T(8,128)(2,1)}), bf16[160,2560]{1,0:T(8,128)(2,1)}) %reduce-scatter.8.cloned.1.call-update) | async-done | bytes 819216 | tf_op jit(solution)/shard_map/reduce_scatter | solution.py:62
  212.9 1.0 slice.47
  213.9 2.9 collective-permute-start.5
  216.8 40.2 %reduce-scatter.10.cloned.1.call-done = bf16[160,2560]{1,0:T(8,128)(2,1)} async-done(((bf16[640,2560]{1,0:T(8,128)(2,1)}), bf16[160,2560]{1,0:T(8,128)(2,1)}) %reduce-scatter.10.cloned.1.call-update) | async-done | bytes 819216 | tf_op jit(solution)/shard_map/reduce_scatter | solution.py:62
  257.0 1.2 slice.51
  258.2 2.8 collective-permute-start.7
  261.0 2.1 fusion.25
  263.1 14.2 %collective-permute-done.7 = bf16[80,2560]{1,0:T(8,128)(2,1)S(1)} collective-permute-done((bf16[80,2560]{1,0:T(8,128)(2,1)S(1)}, bf16[80,2560]{1,0:T(8,128)(2,1)S(1)}, u32[]{:S(2)}, u32[]{:S(2)}) %collective-permute-start.7) | collective-permute-done | bytes 409632 | tf_op jit(solution)/shard_map/ppermute | solution.py:50
  277.2 2.1 fusion.27
  279.3 1.6 fusion.15
  280.9 1.3 copy.57
  282.1 2.5 reshape.185
  284.7 31.8 %reduce-scatter.12.cloned.1.call-done = f32[800,128]{1,0:T(8,128)} async-done(((f32[3200,128]{1,0:T(8,128)}), f32[800,128]{1,0:T(8,128)}) %reduce-scatter.12.cloned.1.call-update) | async-done | bytes 409616 | tf_op jit(solution)/shard_map/reduce_scatter | solution.py:71
  316.6 25.3 %reduce-scatter.14.cloned.1.call-done = f32[200,128]{1,0:T(8,128)} async-done(((f32[800,128]{1,0:T(8,128)}), f32[200,128]{1,0:T(8,128)}) %reduce-scatter.14.cloned.1.call-update) | async-done | bytes 102416
  341.9 15.9 %all_gather.14 = f32[800,128]{1,0:T(8,128)} all-gather(f32[200,128]{1,0:T(8,128)} %reduce-scatter.14.cloned.1.call-done), channel_id=1, replica_groups=mesh['gz'=4,'gy'=4,'fx'=4,'fz'=2,'fc'=2] {'gz'}, dimensions={0}, use_global_device_ids=true | all-gather | bytes 512000 | tf_op jit(solution)/shard_map/all_gather | solution.py:73
  357.9 0.5 fusion.21
  358.4 2.4 copy.58
  360.8 29.9 %all-gather.8.cloned.1.call-done = f32[3200,128]{1,0:T(8,128)} async-done(((f32[800,128]{1,0:T(8,128)}), f32[3200,128]{1,0:T(8,128)}) %all-gather.8.cloned.1.call-update) | async-done | bytes 1638416 | tf_op jit(solution)/shard_map/all_gather | solution.py:73
  390.7 1.5 broadcast_multiply_fusion
  392.2 0.9 mul.220
  393.1 4.8 %multiply_subtract_fusion = (f32[80,2,2560]{2,1,0:T(2,128)}, f32[80,2,2560]{2,1,0:T(2,128)}) fusion(f32[80,2,2560]{2,1,0:T(2,128)} %param.16, f32[80,2,2560]{2,1,0:T(2,128)S(1)} %mul.220, f32[80,2,2560]{2,1,0:T(2,128)} %param.17), kind=kLoop, calls=%fused_computation.43 | loop fusion | flops 2457600 | bytes 8192000 | tf_op jit(solution)/shard_map/sub | solution.py:134
  (50 shorter events, 0.7 us)
Async XLA Ops:
  7.2 70.8 %all-gather.6.cloned.1.call-start = ((), (), s32[]{:S(2)}) async-start(), calls=%async_computation.5 | async-start | bytes 4096000 | tf_op jit(solution)/shard_map/all_gather | solution.py:55
  8.5 36.3 %copy-start.8 = (bf16[1,512,1280]{2,1,0:T(8,128)(2,1)S(1)}, bf16[1,512,1280]{2,1,0:T(8,128)(2,1)}, u32[]{:S(2)}) copy-start(bf16[1,512,1280]{2,1,0:T(8,128)(2,1)} %param.9) | copy-start | bytes 3932164
  8.5 18.5 %collective-permute-start.2 = (bf16[80,2560]{1,0:T(8,128)(2,1)S(1)}, bf16[80,2560]{1,0:T(8,128)(2,1)S(1)}, u32[]{:S(2)}, u32[]{:S(2)}) collective-permute-start(bf16[80,2560]{1,0:T(8,128)(2,1)S(1)} %get-tuple-element.22), channel_id=1, source_target_pairs={{0,2},{2,0},{1,3},{3,1},{4,6},{6,4},{5,7},{7,5},{8,10},{10,8},{9,1... | collective-permute-start | bytes 1228808 | tf_op jit(solution)/shard_map/ppermute | solution.py:50
  27.9 95.9 %all-gather.4.cloned.1.call-start = ((), (), s32[]{:S(2)}) async-start(), calls=%async_computation.4 | async-start | bytes 4096000 | tf_op jit(solution)/shard_map/all_gather | solution.py:55
  28.0 15.7 %collective-permute-start = (bf16[80,2560]{1,0:T(8,128)(2,1)S(1)}, bf16[80,2560]{1,0:T(8,128)(2,1)S(1)}, u32[]{:S(2)}, u32[]{:S(2)}) collective-permute-start(bf16[80,2560]{1,0:T(8,128)(2,1)S(1)} %get-tuple-element.21), channel_id=1, source_target_pairs={{0,2},{2,0},{1,3},{3,1},{4,6},{6,4},{5,7},{7,5},{8,10},{10,8},{9,1... | collective-permute-start | bytes 1228808 | tf_op jit(solution)/shard_map/ppermute | solution.py:50
  44.7 2.7 copy-start.11
  44.7 168.2 %reduce-scatter.8.cloned.1.call-start = ((), (), s32[]{:S(2)}) async-start(), calls=%async_computation.6 | async-start | bytes 4096000 | tf_op jit(solution)/shard_map/reduce_scatter | solution.py:62
  54.8 69.7 %copy-start.12 = (s32[1,4]{1,0:T(1,128)S(1)}, s32[1,4]{1,0:T(1,128)}, u32[]{:S(2)}) copy-start(s32[1,4]{1,0:T(1,128)} %param.12) | copy-start | bytes 52
  78.0 63.9 %collective-permute-start.3 = (bf16[640,2560]{1,0:T(8,128)(2,1)}, bf16[640,2560]{1,0:T(8,128)(2,1)}, u32[]{:S(2)}, u32[]{:S(2)}) collective-permute-start(bf16[640,2560]{1,0:T(8,128)(2,1)} %all-gather.6.cloned.1.call-done), channel_id=1, source_target_pairs={{0,1},{1,0},{2,3},{3,2},{4,5},{5,4},{6,7},{7,6},{8,9},{9,8},{10,11... | collective-permute-start | bytes 9830408 | tf_op jit(solution)/shard_map/ppermute | solution.py:50
  123.8 25.1 %collective-permute-start.1 = (bf16[640,2560]{1,0:T(8,128)(2,1)}, bf16[640,2560]{1,0:T(8,128)(2,1)}, u32[]{:S(2)}, u32[]{:S(2)}) collective-permute-start(bf16[640,2560]{1,0:T(8,128)(2,1)} %all-gather.4.cloned.1.call-done), channel_id=1, source_target_pairs={{0,1},{1,0},{2,3},{3,2},{4,5},{5,4},{6,7},{7,6},{8,9},{9,8},{10,11... | collective-permute-start | bytes 9830408 | tf_op jit(solution)/shard_map/ppermute | solution.py:50
  136.3 2.6 copy-start
  136.3 3.3 copy-start.1
  141.5 1.9 copy-start.9
  143.4 7.9 %copy-start.10 = (bf16[640,2560]{1,0:T(8,128)(2,1)S(1)}, bf16[640,2560]{1,0:T(8,128)(2,1)}, u32[]{:S(2)}) copy-start(bf16[640,2560]{1,0:T(8,128)(2,1)} %all-gather.4.cloned.1.call-done) | copy-start | bytes 9830404
  148.9 2.4 copy-start.13
  162.6 5.9 %collective-permute-start.4 = (bf16[640,2560]{1,0:T(8,128)(2,1)S(1)}, bf16[640,2560]{1,0:T(8,128)(2,1)S(1)}, u32[]{:S(2)}, u32[]{:S(2)}) collective-permute-start(bf16[640,2560]{1,0:T(8,128)(2,1)S(1)} %slice.45), channel_id=1, source_target_pairs={{0,1},{1,0},{2,3},{3,2},{4,5},{5,4},{6,7},{7,6},{8,9},{9,8},{10,11... | collective-permute-start | bytes 9830408 | tf_op jit(solution)/shard_map/ppermute | solution.py:50
  171.1 85.9 %reduce-scatter.10.cloned.1.call-start = ((), (), s32[]{:S(2)}) async-start(), calls=%async_computation.7 | async-start | bytes 4096000 | tf_op jit(solution)/shard_map/reduce_scatter | solution.py:62
  177.3 5.9 %collective-permute-start.6 = (bf16[640,2560]{1,0:T(8,128)(2,1)S(1)}, bf16[640,2560]{1,0:T(8,128)(2,1)S(1)}, u32[]{:S(2)}, u32[]{:S(2)}) collective-permute-start(bf16[640,2560]{1,0:T(8,128)(2,1)S(1)} %slice.49), channel_id=1, source_target_pairs={{0,1},{1,0},{2,3},{3,2},{4,5},{5,4},{6,7},{7,6},{8,9},{9,8},{10,11... | collective-permute-start | bytes 9830408 | tf_op jit(solution)/shard_map/ppermute | solution.py:50
  185.9 130.7 %reduce-scatter.12.cloned.1.call-start = ((), (), s32[]{:S(2)}) async-start(), calls=%async_computation.8 | async-start | bytes 2048000 | tf_op jit(solution)/shard_map/reduce_scatter | solution.py:71
  213.9 47.1 %collective-permute-start.5 = (bf16[80,2560]{1,0:T(8,128)(2,1)S(1)}, bf16[80,2560]{1,0:T(8,128)(2,1)S(1)}, u32[]{:S(2)}, u32[]{:S(2)}) collective-permute-start(bf16[80,2560]{1,0:T(8,128)(2,1)S(1)} %slice.47), channel_id=1, source_target_pairs={{0,2},{2,0},{1,3},{3,1},{4,6},{6,4},{5,7},{7,5},{8,10},{10,8},{9,1... | collective-permute-start | bytes 1228808 | tf_op jit(solution)/shard_map/ppermute | solution.py:50
  257.0 22.3 %copy-start.7 = (f32[1,80,2,2560]{3,2,1,0:T(2,128)S(1)}, f32[1,80,2,2560]{3,2,1,0:T(2,128)}, u32[]{:S(2)}) copy-start(f32[1,80,2,2560]{3,2,1,0:T(2,128)} %param.15) | copy-start | bytes 4915204
  258.1 21.2 %copy-start.2 = (f32[1,80,2,2560]{3,2,1,0:T(2,128)S(1)}, f32[1,80,2,2560]{3,2,1,0:T(2,128)}, u32[]{:S(2)}) copy-start(f32[1,80,2,2560]{3,2,1,0:T(2,128)} %param.14) | copy-start | bytes 4915204
  258.2 21.1 %copy-start.3 = (f32[80,2,2560]{2,1,0:T(2,128)S(1)}, f32[80,2,2560]{2,1,0:T(2,128)}, u32[]{:S(2)}) copy-start(f32[80,2,2560]{2,1,0:T(2,128)} %param.16) | copy-start | bytes 4915204
  258.2 21.1 %copy-start.4 = (bf16[1,80,2,2560]{3,2,1,0:T(2,128)(2,1)S(1)}, bf16[1,80,2,2560]{3,2,1,0:T(2,128)(2,1)}, u32[]{:S(2)}) copy-start(bf16[1,80,2,2560]{3,2,1,0:T(2,128)(2,1)} %param.13) | copy-start | bytes 2457604
  258.2 19.1 %collective-permute-start.7 = (bf16[80,2560]{1,0:T(8,128)(2,1)S(1)}, bf16[80,2560]{1,0:T(8,128)(2,1)S(1)}, u32[]{:S(2)}, u32[]{:S(2)}) collective-permute-start(bf16[80,2560]{1,0:T(8,128)(2,1)S(1)} %slice.51), channel_id=1, source_target_pairs={{0,2},{2,0},{1,3},{3,1},{4,6},{6,4},{5,7},{7,5},{8,10},{10,8},{9,1... | collective-permute-start | bytes 1228808 | tf_op jit(solution)/shard_map/ppermute | solution.py:50
  284.6 73.2 %copy-start.5 = (f32[1,80,1,2560]{3,1,2,0:T(8,128)S(1)}, f32[1,80,1,2560]{3,1,2,0:T(8,128)}, u32[]{:S(2)}) copy-start(f32[1,80,1,2560]{3,1,2,0:T(8,128)} %get-tuple-element.18) | copy-start | bytes 2457604
  284.6 73.3 %copy-start.6 = (f32[1,80,1,2560]{3,1,2,0:T(8,128)S(1)}, f32[1,80,1,2560]{3,1,2,0:T(8,128)}, u32[]{:S(2)}) copy-start(f32[1,80,1,2560]{3,1,2,0:T(8,128)} %get-tuple-element.20) | copy-start | bytes 2457604
  284.6 57.3 %reduce-scatter.14.cloned.1.call-start = ((), (), s32[]{:S(2)}) async-start(), calls=%async_computation.10 | async-start | bytes 512000
  316.6 74.1 %all-gather.8.cloned.1.call-start = ((), (), s32[]{:S(2)}) async-start(), calls=%async_computation.9 | async-start | bytes 2048000 | tf_op jit(solution)/shard_map/all_gather | solution.py:73
Sparse Core Ops, SparseCore 0:
  28.1 49.8 all-gather.5
  80.4 43.3 all-gather.3
  171.2 41.6 reduce-scatter.7
  215.3 41.6 reduce-scatter.9
  284.8 31.7 reduce-scatter.11
  319.1 22.8 reduce-scatter.13
  358.0 32.6 all-gather.7

commit v3 on v2

--- a/solution.py
+++ b/solution.py
@@ -43,7 +43,7 @@
     split = columns.reshape(rows, sizes["fx"], sizes["fz"], sizes["fc"], local)
     split = jnp.where(lax.axis_index("fz") == 0, split, jnp.flip(split, axis=2))
     split = jnp.where(lax.axis_index("fc") == 0, split, jnp.flip(split, axis=3))
-    return jnp.transpose(split, (0, 3, 1, 2, 4)).reshape(columns.shape)
+    return jnp.transpose(split, (0, 3, 2, 1, 4)).reshape(columns.shape)
 
 
 def swap(block, name):
@@ -51,26 +51,38 @@
 
 
 def gather_rows(block):
-    block = jnp.concatenate([block, swap(block, "fz")], axis=0)
-    block = lax.all_gather(block, "fx", axis=0, tiled=True)
+    own = lax.all_gather(block, "fx", axis=0, tiled=True)
+    partner = lax.all_gather(swap(block, "fz"), "fx", axis=0, tiled=True)
+    block = jnp.concatenate([own, partner], axis=0)
     return jnp.concatenate([block, swap(block, "fc")], axis=0)
 
 
 def scatter_rows(block):
     half = block.shape[0] // 2
     block = block[:half].astype(jnp.float32) + swap(block[half:], "fc").astype(jnp.float32)
-    block = lax.psum_scatter(block.astype(jnp.bfloat16), "fx", scatter_dimension=0, tiled=True)
+    block = block.astype(jnp.bfloat16)
     half = block.shape[0] // 2
-    return block[:half].astype(jnp.float32) + swap(block[half:], "fz").astype(jnp.float32)
+    partner = lax.psum_scatter(block[half:], "fx", scatter_dimension=0, tiled=True)
+    partner = swap(partner, "fz")
+    own = lax.psum_scatter(block[:half], "fx", scatter_dimension=0, tiled=True)
+    return own.astype(jnp.float32) + partner.astype(jnp.float32)
+
+
+def exchange_add(values, name, size, stride):
+    pairs = [(index, index ^ stride) for index in range(size)]
+    return values + lax.ppermute(values, name, perm=pairs)
 
 
 def group_sum(values):
+    sizes = dict(GROUP_PARTS)
     shape = values.shape
     flat = values.reshape(-1, 128)
-    for name in reversed(GROUP_AXES):
-        flat = lax.psum_scatter(flat, name, scatter_dimension=0, tiled=True)
-    for name in GROUP_AXES:
-        flat = lax.all_gather(flat, name, axis=0, tiled=True)
+    flat = lax.psum_scatter(flat, "gy", scatter_dimension=0, tiled=True)
+    stride = 1
+    while stride < sizes["gz"]:
+        flat = exchange_add(flat, "gz", sizes["gz"], stride)
+        stride *= 2
+    flat = lax.all_gather(flat, "gy", axis=0, tiled=True)
     return flat.reshape(shape)
 
 

time: 409 us -> 428 us (1.046)
  waiting for transfers between devices: 270 us -> 293 us
  blocking collectives: 15.9 us -> 0 us
  other arithmetic: 28.4 us -> 35.2 us
  local copies, waits for them, and re-layouts: 35.6 us -> 40.8 us
    reduce_scatter x3 -> x5, waiting for transfers between devices: 99 us -> 132 us  [the longest x2 57.7 us: scatter_rows(): own = lax.psum_scatter(block[:half], 'fx', scatter_dimension=0, tiled=True)]
    ppermute x0 -> x2, waiting for transfers between devices: none -> 30.9 us  [exchange_add(): return values + lax.ppermute(values, name, perm=pairs)]
    ppermute x8, waiting for transfers between devices: 49.4 us -> 25.7 us  [swap(): return lax.ppermute(block, name, perm=[(0, 1), (1, 0)])]
    unnamed x8 -> x10, waiting for transfers between devices: 25.4 us -> 2.19 us
    all_gather x1 -> x0, blocking collectives: 15.9 us -> none  [group_sum(): flat = lax.all_gather(flat, name, axis=0, tiled=True)]
    all_gather x3 -> x5, waiting for transfers between devices: 95.9 us -> 103 us  [the longest x2 49.6 us: gather_rows(): partner = lax.all_gather(swap(block, 'fz'), 'fx', axis=0, tiled=True)]
    concatenate x2, other arithmetic: 1.89 us -> 8 us  [gather_rows(): block = jnp.concatenate([own, partner], axis=0)]
    slice x0 -> x3, local copies, waits for them, and re-layouts: none -> 4.85 us  [the longest x2 3.84 us: scatter_rows(): own = lax.psum_scatter(block[:half], 'fx', scatter_dimension=0, tiled=True)]
  transfers between devices with their start and end apart: 15 -> 20, of which waited for: 12 -> 14; matrix products, arithmetic and copies ran while one was open for 13% -> 14% of each run, Pallas kernels for 0% -> 0%
where the time goes in v3:
time: 428 us; the launch traced here: 424 us
  waiting for transfers between devices  293 us (68%)
  local copies, waits for them, and re-layouts  40.8 us (10%)
  other arithmetic  35.2 us (8%)
  matrix products  20.6 us (5%)
  starting transfers between devices  19.4 us (5%)
  between operations  14.5 us (3%)
    reduce_scatter x2, waiting for transfers between devices, scatter_rows(): own = lax.psum_scatter(block[:half], 'fx', scatter_dimension=0, tiled=True)  57.7 us
    all_gather x2, waiting for transfers between devices, gather_rows(): partner = lax.all_gather(swap(block, 'fz'), 'fx', axis=0, tiled=True)  49.6 us
    reduce_scatter x2, waiting for transfers between devices, scatter_rows(): lax.psum_scatter(block[half:], 'fx', scatter_dimension=0, tiled=True)  47.2 us
    ppermute x2, waiting for transfers between devices, exchange_add(): return values + lax.ppermute(values, name, perm=pairs)  30.9 us
    reduce_scatter x1, waiting for transfers between devices, group_sum(): flat = lax.psum_scatter(flat, 'gy', scatter_dimension=0, tiled=True)  27.2 us
    all_gather x2, waiting for transfers between devices, gather_rows(): own = lax.all_gather(block, 'fx', axis=0, tiled=True)  26.7 us
    all_gather x1, waiting for transfers between devices, group_sum(): flat = lax.all_gather(flat, 'gy', axis=0, tiled=True)  26.3 us
    ppermute x8, waiting for transfers between devices, swap(): return lax.ppermute(block, name, perm=[(0, 1), (1, 0)])  25.7 us
  transfers between devices with their start and end apart: 20, of which 14 were waited for; matrix products, arithmetic and copies ran while one was open for 14% of the time, Pallas kernels for 0%

profile of v3, /device:TPU:121, one launch (start us, length us, event | category | flops | bytes accessed | tf_op | source)
XLA Modules:
  0.0 423.9 jit_solution(16115290313522838295)
XLA Ops:
  7.2 1.3 copy.37
  8.5 1.0 fusion.41
  9.6 4.3 %collective-permute-start.2 = (bf16[80,2560]{1,0:T(8,128)(2,1)S(1)}, bf16[80,2560]{1,0:T(8,128)(2,1)S(1)}, u32[]{:S(2)}, u32[]{:S(2)}) collective-permute-start(bf16[80,2560]{1,0:T(8,128)(2,1)S(1)} %get-tuple-element.23), channel_id=1, source_target_pairs={{0,2},{2,0},{1,3},{3,1},{4,6},{6,4},{5,7},{7,5},{8,10},{10,8},{9,1... | collective-permute-start | bytes 1228808 | tf_op jit(solution)/shard_map/ppermute | solution.py:50
  13.9 14.2 %collective-permute-done.2 = bf16[80,2560]{1,0:T(8,128)(2,1)S(1)} collective-permute-done((bf16[80,2560]{1,0:T(8,128)(2,1)S(1)}, bf16[80,2560]{1,0:T(8,128)(2,1)S(1)}, u32[]{:S(2)}, u32[]{:S(2)}) %collective-permute-start.2) | collective-permute-done | bytes 409632 | tf_op jit(solution)/shard_map/ppermute | solution.py:50
  28.1 0.7 copy-done.15
  28.9 0.7 all-gather.14.cloned.1.call-update
  29.6 6.2 %collective-permute-start = (bf16[80,2560]{1,0:T(8,128)(2,1)S(1)}, bf16[80,2560]{1,0:T(8,128)(2,1)S(1)}, u32[]{:S(2)}, u32[]{:S(2)}) collective-permute-start(bf16[80,2560]{1,0:T(8,128)(2,1)S(1)} %get-tuple-element.24), channel_id=1, source_target_pairs={{0,2},{2,0},{1,3},{3,1},{4,6},{6,4},{5,7},{7,5},{8,10},{10,8},{9,1... | collective-permute-start | bytes 1228808 | tf_op jit(solution)/shard_map/ppermute | solution.py:50
  35.8 8.8 %collective-permute-done = bf16[80,2560]{1,0:T(8,128)(2,1)S(1)} collective-permute-done((bf16[80,2560]{1,0:T(8,128)(2,1)S(1)}, bf16[80,2560]{1,0:T(8,128)(2,1)S(1)}, u32[]{:S(2)}, u32[]{:S(2)}) %collective-permute-start) | collective-permute-done | bytes 409632 | tf_op jit(solution)/shard_map/ppermute | solution.py:50
  44.6 0.8 copy-done.16
  45.5 0.7 copy.30
  46.1 1.8 copy.31
  48.0 3.9 gather_fusion
  51.9 3.2 copy.33
  55.2 18.4 %all-gather.10.cloned.1.call-done = bf16[320,2560]{1,0:T(8,128)(2,1)} async-done(((bf16[80,2560]{1,0:T(8,128)(2,1)}), bf16[320,2560]{1,0:T(8,128)(2,1)}) %all-gather.10.cloned.1.call-update) | async-done | bytes 1638416 | tf_op jit(solution)/shard_map/all_gather | solution.py:55
  73.6 4.1 pad_maximum_fusion.1
  77.7 0.7 collective-permute-start.3
  78.4 0.5 fusion.28
  78.9 26.7 %all-gather.14.cloned.1.call-done = bf16[1,320,1,2560]{3,1,2,0:T(8,128)(2,1)} async-done(((bf16[1,80,1,2560]{3,1,2,0:T(8,128)(2,1)}), bf16[1,320,1,2560]{3,1,2,0:T(8,128)(2,1)}) %all-gather.14.cloned.1.call-update) | async-done | bytes 1638416 | tf_op jit(solution)/shard_map/all_gather | solution.py:54
  105.6 31.3 %all-gather.8.cloned.1.call-done = bf16[320,2560]{1,0:T(8,128)(2,1)} async-done(((bf16[80,2560]{1,0:T(8,128)(2,1)}), bf16[320,2560]{1,0:T(8,128)(2,1)}) %all-gather.8.cloned.1.call-update) | async-done | bytes 1638416 | tf_op jit(solution)/shard_map/all_gather | solution.py:55
  136.8 3.9 pad_maximum_fusion
  140.7 0.7 collective-permute-start.1
  141.5 4.1 copy.32
  145.6 1.9 convert_element_type.103
  147.5 4.1 gather.9
  151.6 1.6 copy.35
  153.2 2.5 multiply_reduce_fusion
  155.8 0.7 copy-done.2
  156.5 0.7 multiply_convert_fusion.3
  157.3 0.7 reverse_select_fusion.1
  158.8 1.0 copy-done.10
  160.3 5.5 %fusion.8 = f32[512,2560]{1,0:T(8,128)S(1)} fusion(bf16[512,1280]{0,1:T(8,128)(2,1)S(1)} %bitcast.61, bf16[640,2560]{1,0:T(8,128)(2,1)} %collective-permute-done.3, bf16[320,2560]{1,0:T(8,128)(2,1)S(1)} %copy-done.11, bf16[320,2560]{1,0:T(8,128)(2,1)S(1)} %bitcast.56), kind=kOutput, calls=%fused_computation.11 | convolution fusion | flops 3375104000 | bytes 13107200 | tf_op jit(solution)/shard_map/dot_general | solution.py:116
  165.8 7.3 %multiply_convert_fusion.1 = bf16[512,2560]{1,0:T(8,128)(2,1)S(1)} fusion(f32[512,2560]{1,0:T(8,128)S(1)} %fusion.8, bf16[512,1280]{0,1:T(8,128)(2,1)S(1)} %bitcast.59, bf16[640,2560]{1,0:T(8,128)(2,1)} %collective-permute-done.1, bf16[320,2560]{1,0:T(8,128)(2,1)S(1)} %copy-done.13, bf16[320,2560]{1,0:T(8,128)(2,1)S(1)} %bitcast.58), kind=kOutput, calls=%fused_computation.20 | convolution fusion | flops 3390832640 | bytes 15728640 | tf_op jit(solution)/shard_map/dot_general | solution.py:125
  173.2 3.8 fusion
  177.5 4.0 fusion.1
  181.5 2.1 slice.49
  183.6 1.7 copy-done.3
  185.8 0.9 add_convert_fusion.1
  186.7 1.9 fusion.39
  188.7 2.8 collective-permute-done.6
  191.5 2.7 add_convert_fusion
  194.3 1.9 fusion.40
  196.3 0.7 reduce-scatter.6.cloned.1.call-update
  197.0 0.7 reduce-scatter.10.cloned.1.call-update
  197.8 18.6 %reduce-scatter.8.cloned.1.call-done = bf16[80,2560]{1,0:T(8,128)(2,1)} async-done(((bf16[320,2560]{1,0:T(8,128)(2,1)}), bf16[80,2560]{1,0:T(8,128)(2,1)}) %reduce-scatter.8.cloned.1.call-update) | async-done | bytes 409616 | tf_op jit(solution)/shard_map/reduce_scatter | solution.py:65
  216.4 2.9 collective-permute-start.5
  219.3 28.6 %reduce-scatter.12.cloned.1.call-done = bf16[80,2560]{1,0:T(8,128)(2,1)} async-done(((bf16[320,2560]{1,0:T(8,128)(2,1)}), bf16[80,2560]{1,0:T(8,128)(2,1)}) %reduce-scatter.12.cloned.1.call-update) | async-done | bytes 409616 | tf_op jit(solution)/shard_map/reduce_scatter | solution.py:65
  247.9 2.9 collective-permute-start.7
  250.7 28.6 %reduce-scatter.6.cloned.1.call-done = bf16[80,2560]{1,0:T(8,128)(2,1)} async-done(((bf16[320,2560]{1,0:T(8,128)(2,1)}), bf16[80,2560]{1,0:T(8,128)(2,1)}) %reduce-scatter.6.cloned.1.call-update) | async-done | bytes 409616 | tf_op jit(solution)/shard_map/reduce_scatter | solution.py:67
  279.3 2.5 fusion.29
  281.8 29.1 %reduce-scatter.10.cloned.1.call-done = bf16[80,2560]{1,0:T(8,128)(2,1)} async-done(((bf16[320,2560]{1,0:T(8,128)(2,1)}), bf16[80,2560]{1,0:T(8,128)(2,1)}) %reduce-scatter.10.cloned.1.call-update) | async-done | bytes 409616 | tf_op jit(solution)/shard_map/reduce_scatter | solution.py:67
  310.9 2.3 fusion.31
  313.2 3.0 fusion.19
  316.2 1.3 copy.42
  317.5 2.5 reshape.185
  320.0 27.2 %reduce-scatter.14.cloned.1.call-done = f32[800,128]{1,0:T(8,128)} async-done(((f32[3200,128]{1,0:T(8,128)}), f32[800,128]{1,0:T(8,128)}) %reduce-scatter.14.cloned.1.call-update) | async-done | bytes 409616 | tf_op jit(solution)/shard_map/reduce_scatter | solution.py:80
  347.4 10.0 %collective-permute-done.8 = f32[800,128]{1,0:T(8,128)S(1)} collective-permute-done((f32[800,128]{1,0:T(8,128)}, f32[800,128]{1,0:T(8,128)S(1)}, u32[]{:S(2)}, u32[]{:S(2)}) %collective-permute-start.8) | collective-permute-done | bytes 409632 | tf_op jit(solution)/shard_map/ppermute | solution.py:73
  357.4 1.1 add.114
  358.9 20.9 %collective-permute-done.9 = f32[800,128]{1,0:T(8,128)S(1)} collective-permute-done((f32[800,128]{1,0:T(8,128)S(1)}, f32[800,128]{1,0:T(8,128)S(1)}, u32[]{:S(2)}, u32[]{:S(2)}) %collective-permute-start.9) | collective-permute-done | bytes 409632 | tf_op jit(solution)/shard_map/ppermute | solution.py:73
  379.8 0.8 add.115
  381.1 2.4 copy.43
  383.6 26.3 %all-gather.12.cloned.1.call-done = f32[3200,128]{1,0:T(8,128)} async-done(((f32[800,128]{1,0:T(8,128)}), f32[3200,128]{1,0:T(8,128)}) %all-gather.12.cloned.1.call-update) | async-done | bytes 1638416 | tf_op jit(solution)/shard_map/all_gather | solution.py:85
  409.9 1.5 broadcast_multiply_fusion
  411.4 0.9 mul.220
  412.3 4.8 %multiply_subtract_fusion = (f32[80,2,2560]{2,1,0:T(2,128)}, f32[80,2,2560]{2,1,0:T(2,128)}) fusion(f32[80,2,2560]{2,1,0:T(2,128)} %param.16, f32[80,2,2560]{2,1,0:T(2,128)S(1)} %mul.220, f32[80,2,2560]{2,1,0:T(2,128)} %param.17), kind=kLoop, calls=%fused_computation.49 | loop fusion | flops 2457600 | bytes 8192000 | tf_op jit(solution)/shard_map/sub | solution.py:146
  (74 shorter events, 4.3 us)
Async XLA Ops:
  7.2 38.3 %copy-start.14 = (bf16[1,512,1280]{2,1,0:T(8,128)(2,1)S(1)}, bf16[1,512,1280]{2,1,0:T(8,128)(2,1)}, u32[]{:S(2)}) copy-start(bf16[1,512,1280]{2,1,0:T(8,128)(2,1)} %param.9) | copy-start | bytes 3932164
  7.2 48.1 %all-gather.16.cloned.1.call-start = ((), (), s32[]{:S(2)}) async-start(), calls=%async_computation.14 | async-start | bytes 2048000 | tf_op jit(solution)/shard_map/all_gather | solution.py:54
  9.6 64.0 %all-gather.10.cloned.1.call-start = ((), (), s32[]{:S(2)}) async-start(), calls=%async_computation.6 | async-start | bytes 2048000 | tf_op jit(solution)/shard_map/all_gather | solution.py:55
  9.6 18.5 %collective-permute-start.2 = (bf16[80,2560]{1,0:T(8,128)(2,1)S(1)}, bf16[80,2560]{1,0:T(8,128)(2,1)S(1)}, u32[]{:S(2)}, u32[]{:S(2)}) collective-permute-start(bf16[80,2560]{1,0:T(8,128)(2,1)S(1)} %get-tuple-element.23), channel_id=1, source_target_pairs={{0,2},{2,0},{1,3},{3,1},{4,6},{6,4},{5,7},{7,5},{8,10},{10,8},{9,1... | collective-permute-start | bytes 1228808 | tf_op jit(solution)/shard_map/ppermute | solution.py:50
  28.1 0.8 copy-start.15
  28.9 76.7 %all-gather.14.cloned.1.call-start = ((), (), s32[]{:S(2)}) async-start(), calls=%async_computation.13 | async-start | bytes 2048000 | tf_op jit(solution)/shard_map/all_gather | solution.py:54
  29.6 107.2 %all-gather.8.cloned.1.call-start = ((), (), s32[]{:S(2)}) async-start(), calls=%async_computation.5 | async-start | bytes 2048000 | tf_op jit(solution)/shard_map/all_gather | solution.py:55
  29.6 15.0 %collective-permute-start = (bf16[80,2560]{1,0:T(8,128)(2,1)S(1)}, bf16[80,2560]{1,0:T(8,128)(2,1)S(1)}, u32[]{:S(2)}, u32[]{:S(2)}) collective-permute-start(bf16[80,2560]{1,0:T(8,128)(2,1)S(1)} %get-tuple-element.24), channel_id=1, source_target_pairs={{0,2},{2,0},{1,3},{3,1},{4,6},{6,4},{5,7},{7,5},{8,10},{10,8},{9,1... | collective-permute-start | bytes 1228808 | tf_op jit(solution)/shard_map/ppermute | solution.py:50
  44.6 0.8 copy-start.16
  45.4 2.6 copy-start.17
  45.4 171.0 %reduce-scatter.8.cloned.1.call-start = ((), (), s32[]{:S(2)}) async-start(), calls=%async_computation.8 | async-start | bytes 2048000 | tf_op jit(solution)/shard_map/reduce_scatter | solution.py:65
  73.6 4.8 %copy-start = (f32[1,512,1280]{1,2,0:T(8,128)S(1)}, f32[1,512,1280]{1,2,0:T(8,128)}, u32[]{:S(2)}) copy-start(f32[1,512,1280]{1,2,0:T(8,128)} %copy.33) | copy-start | bytes 7864324
  77.7 81.1 %collective-permute-start.3 = (bf16[640,2560]{1,0:T(8,128)(2,1)}, bf16[640,2560]{1,0:T(8,128)(2,1)}, u32[]{:S(2)}, u32[]{:S(2)}) collective-permute-start(bf16[640,2560]{1,0:T(8,128)(2,1)} %pad_maximum_fusion.1), channel_id=1, source_target_pairs={{0,1},{1,0},{2,3},{3,2},{4,5},{5,4},{6,7},{7,6},{8,9},{9,8},{10,11... | collective-permute-start | bytes 9830408 | tf_op jit(solution)/shard_map/ppermute | solution.py:50
  136.8 4.6 %copy-start.18 = (s32[1,4]{1,0:T(1,128)S(1)}, s32[1,4]{1,0:T(1,128)}, u32[]{:S(2)}) copy-start(s32[1,4]{1,0:T(1,128)} %param.12) | copy-start | bytes 52
  140.7 25.1 %collective-permute-start.1 = (bf16[640,2560]{1,0:T(8,128)(2,1)}, bf16[640,2560]{1,0:T(8,128)(2,1)}, u32[]{:S(2)}, u32[]{:S(2)}) collective-permute-start(bf16[640,2560]{1,0:T(8,128)(2,1)} %pad_maximum_fusion), channel_id=1, source_target_pairs={{0,1},{1,0},{2,3},{3,2},{4,5},{5,4},{6,7},{7,6},{8,9},{9,8},{10,11... | collective-permute-start | bytes 9830408 | tf_op jit(solution)/shard_map/ppermute | solution.py:50
  153.2 2.6 copy-start.1
  153.2 3.3 copy-start.2
  158.4 1.4 copy-start.10
  158.4 1.9 copy-start.11
  160.3 5.5 %copy-start.12 = (bf16[1,320,1,2560]{3,1,2,0:T(8,128)(2,1)S(1)}, bf16[1,320,1,2560]{3,1,2,0:T(8,128)(2,1)}, u32[]{:S(2)}) copy-start(bf16[1,320,1,2560]{3,1,2,0:T(8,128)(2,1)} %all-gather.14.cloned.1.call-done) | copy-start | bytes 4915204
  160.3 5.5 %copy-start.13 = (bf16[320,2560]{1,0:T(8,128)(2,1)S(1)}, bf16[320,2560]{1,0:T(8,128)(2,1)}, u32[]{:S(2)}) copy-start(bf16[320,2560]{1,0:T(8,128)(2,1)} %all-gather.8.cloned.1.call-done) | copy-start | bytes 4915204
  177.2 8.6 %collective-permute-start.4 = (bf16[640,2560]{1,0:T(8,128)(2,1)S(1)}, bf16[640,2560]{1,0:T(8,128)(2,1)S(1)}, u32[]{:S(2)}, u32[]{:S(2)}) collective-permute-start(bf16[640,2560]{1,0:T(8,128)(2,1)S(1)} %slice.45), channel_id=1, source_target_pairs={{0,1},{1,0},{2,3},{3,2},{4,5},{5,4},{6,7},{7,6},{8,9},{9,8},{10,11... | collective-permute-start | bytes 9830408 | tf_op jit(solution)/shard_map/ppermute | solution.py:50
  181.5 3.9 copy-start.3
  185.4 6.2 %collective-permute-start.6 = (bf16[640,2560]{1,0:T(8,128)(2,1)}, bf16[640,2560]{1,0:T(8,128)(2,1)S(1)}, u32[]{:S(2)}, u32[]{:S(2)}) collective-permute-start(bf16[640,2560]{1,0:T(8,128)(2,1)} %slice.49), channel_id=1, source_target_pairs={{0,1},{1,0},{2,3},{3,2},{4,5},{5,4},{6,7},{7,6},{8,9},{9,8},{10,11... | collective-permute-start | bytes 9830408 | tf_op jit(solution)/shard_map/ppermute | solution.py:50
  188.7 59.2 %reduce-scatter.12.cloned.1.call-start = ((), (), s32[]{:S(2)}) async-start(), calls=%async_computation.10 | async-start | bytes 2048000 | tf_op jit(solution)/shard_map/reduce_scatter | solution.py:65
  196.2 83.1 %reduce-scatter.6.cloned.1.call-start = ((), (), s32[]{:S(2)}) async-start(), calls=%async_computation.7 | async-start | bytes 2048000 | tf_op jit(solution)/shard_map/reduce_scatter | solution.py:67
  197.0 113.9 %reduce-scatter.10.cloned.1.call-start = ((), (), s32[]{:S(2)}) async-start(), calls=%async_computation.9 | async-start | bytes 2048000 | tf_op jit(solution)/shard_map/reduce_scatter | solution.py:67
  197.7 115.5 %copy-start.4 = (f32[1,80,2,2560]{3,2,1,0:T(2,128)S(1)}, f32[1,80,2,2560]{3,2,1,0:T(2,128)}, u32[]{:S(2)}) copy-start(f32[1,80,2,2560]{3,2,1,0:T(2,128)} %param.14) | copy-start | bytes 4915204
  197.7 115.5 %copy-start.5 = (f32[80,2,2560]{2,1,0:T(2,128)S(1)}, f32[80,2,2560]{2,1,0:T(2,128)}, u32[]{:S(2)}) copy-start(f32[80,2,2560]{2,1,0:T(2,128)} %param.16) | copy-start | bytes 4915204
  197.7 149.5 %reduce-scatter.14.cloned.1.call-start = ((), (), s32[]{:S(2)}) async-start(), calls=%async_computation.11 | async-start | bytes 2048000 | tf_op jit(solution)/shard_map/reduce_scatter | solution.py:80
  216.4 62.9 %collective-permute-start.5 = (bf16[80,2560]{1,0:T(8,128)(2,1)}, bf16[80,2560]{1,0:T(8,128)(2,1)}, u32[]{:S(2)}, u32[]{:S(2)}) collective-permute-start(bf16[80,2560]{1,0:T(8,128)(2,1)} %reduce-scatter.8.cloned.1.call-done), channel_id=1, source_target_pairs={{0,2},{2,0},{1,3},{3,1},{4,6},{6,4},{5,7},{7,5},{8,10},{10,8},{9,1... | collective-permute-start | bytes 1228808 | tf_op jit(solution)/shard_map/ppermute | solution.py:50
  247.9 63.0 %collective-permute-start.7 = (bf16[80,2560]{1,0:T(8,128)(2,1)}, bf16[80,2560]{1,0:T(8,128)(2,1)}, u32[]{:S(2)}, u32[]{:S(2)}) collective-permute-start(bf16[80,2560]{1,0:T(8,128)(2,1)} %reduce-scatter.12.cloned.1.call-done), channel_id=1, source_target_pairs={{0,2},{2,0},{1,3},{3,1},{4,6},{6,4},{5,7},{7,5},{8,10},{10,8},{9,1... | collective-permute-start | bytes 1228808 | tf_op jit(solution)/shard_map/ppermute | solution.py:50
  310.9 2.3 copy-start.6
  310.9 2.3 copy-start.9
  319.9 60.7 %copy-start.7 = (f32[1,80,1,2560]{3,1,2,0:T(8,128)S(1)}, f32[1,80,1,2560]{3,1,2,0:T(8,128)}, u32[]{:S(2)}) copy-start(f32[1,80,1,2560]{3,1,2,0:T(8,128)} %get-tuple-element.19) | copy-start | bytes 2457604
  319.9 60.7 %copy-start.8 = (f32[1,80,1,2560]{3,1,2,0:T(8,128)S(1)}, f32[1,80,1,2560]{3,1,2,0:T(8,128)}, u32[]{:S(2)}) copy-start(f32[1,80,1,2560]{3,1,2,0:T(8,128)} %get-tuple-element.21) | copy-start | bytes 2457604
  320.0 89.9 %all-gather.12.cloned.1.call-start = ((), (), s32[]{:S(2)}) async-start(), calls=%async_computation.12 | async-start | bytes 2048000 | tf_op jit(solution)/shard_map/all_gather | solution.py:85
  347.2 10.2 %collective-permute-start.8 = (f32[800,128]{1,0:T(8,128)}, f32[800,128]{1,0:T(8,128)S(1)}, u32[]{:S(2)}, u32[]{:S(2)}) collective-permute-start(f32[800,128]{1,0:T(8,128)} %reduce-scatter.14.cloned.1.call-done), channel_id=1, source_target_pairs={{0,64},{64,0},{128,192},{192,128},{1,65},{65,1},{129,193},{193,129... | collective-permute-start | bytes 1228808 | tf_op jit(solution)/shard_map/ppermute | solution.py:73
  358.5 21.3 %collective-permute-start.9 = (f32[800,128]{1,0:T(8,128)S(1)}, f32[800,128]{1,0:T(8,128)S(1)}, u32[]{:S(2)}, u32[]{:S(2)}) collective-permute-start(f32[800,128]{1,0:T(8,128)S(1)} %add.114), channel_id=1, source_target_pairs={{0,128},{64,192},{128,0},{192,64},{1,129},{65,193},{129,1},{193,65... | collective-permute-start | bytes 1228808 | tf_op jit(solution)/shard_map/ppermute | solution.py:73
Sparse Core Ops, SparseCore 0:
  10.4 31.1 all-gather.15
  44.0 29.5 all-gather.9
  76.0 29.5 all-gather.13
  107.2 29.5 all-gather.7
  188.8 27.5 reduce-scatter.7
  219.6 28.2 reduce-scatter.11
  251.0 28.2 reduce-scatter.5
  282.6 28.2 reduce-scatter.9
  320.1 27.0 reduce-scatter.13
  380.7 29.0 all-gather.11

commit v4 on v3

--- a/solution.py
+++ b/solution.py
@@ -43,7 +43,7 @@
     split = columns.reshape(rows, sizes["fx"], sizes["fz"], sizes["fc"], local)
     split = jnp.where(lax.axis_index("fz") == 0, split, jnp.flip(split, axis=2))
     split = jnp.where(lax.axis_index("fc") == 0, split, jnp.flip(split, axis=3))
-    return jnp.transpose(split, (0, 3, 2, 1, 4)).reshape(columns.shape)
+    return jnp.transpose(split, (0, 3, 1, 2, 4)).reshape(columns.shape)
 
 
 def swap(block, name):
@@ -51,21 +51,17 @@
 
 
 def gather_rows(block):
-    own = lax.all_gather(block, "fx", axis=0, tiled=True)
-    partner = lax.all_gather(swap(block, "fz"), "fx", axis=0, tiled=True)
-    block = jnp.concatenate([own, partner], axis=0)
+    block = jnp.concatenate([block, swap(block, "fz")], axis=0)
+    block = lax.all_gather(block, "fx", axis=0, tiled=True)
     return jnp.concatenate([block, swap(block, "fc")], axis=0)
 
 
 def scatter_rows(block):
     half = block.shape[0] // 2
     block = block[:half].astype(jnp.float32) + swap(block[half:], "fc").astype(jnp.float32)
-    block = block.astype(jnp.bfloat16)
+    block = lax.psum_scatter(block.astype(jnp.bfloat16), "fx", scatter_dimension=0, tiled=True)
     half = block.shape[0] // 2
-    partner = lax.psum_scatter(block[half:], "fx", scatter_dimension=0, tiled=True)
-    partner = swap(partner, "fz")
-    own = lax.psum_scatter(block[:half], "fx", scatter_dimension=0, tiled=True)
-    return own.astype(jnp.float32) + partner.astype(jnp.float32)
+    return block[:half].astype(jnp.float32) + swap(block[half:], "fz").astype(jnp.float32)
 
 
 def exchange_add(values, name, size, stride):
@@ -112,25 +108,21 @@
     normed = gathered_order(normed)
     masked_grad = gathered_order(masked_grad)
 
-    w_in = gather_rows(inner_params[0, :, 0, :])
+    weights = gather_rows(inner_params[0])
+    w_in = weights[:, 0, :]
+    w_out = weights[:, 1, :]
     pre_act = jnp.dot(normed, w_in, preferred_element_type=jnp.float32) * model_width ** (-0.5)
-    cumulative = 0.5 * (1.0 + jax.scipy.special.erf(pre_act * inv_root_two))
-    activation = (pre_act * cumulative).astype(jnp.bfloat16)
+    back_grad = jnp.dot(masked_grad, w_out, preferred_element_type=jnp.float32) * hidden_width ** (-0.5)
+    activation, derivative = gelu_parts(pre_act)
+    activation = activation.astype(jnp.bfloat16)
+    hidden_grad = (back_grad * derivative).astype(jnp.bfloat16)
+    grad_in = lax.dot_general(
+        normed, hidden_grad, (((0,), (0,)), ((), ())), preferred_element_type=jnp.float32
+    ) * model_width ** (-0.5)
     grad_out = lax.dot_general(
         masked_grad, activation, (((0,), (0,)), ((), ())), preferred_element_type=jnp.float32
     ) * hidden_width ** (-0.5)
-    grad_out = scatter_rows(grad_out.astype(jnp.bfloat16))
-
-    w_out = gather_rows(inner_params[0, :, 1, :])
-    back_grad = jnp.dot(masked_grad, w_out, preferred_element_type=jnp.float32) * hidden_width ** (-0.5)
-    density = jnp.exp(-0.5 * pre_act * pre_act) * inv_root_tau
-    hidden_grad = (back_grad * (cumulative + pre_act * density)).astype(jnp.bfloat16)
-    grad_in = lax.dot_general(
-        normed, hidden_grad, (((0,), (0,)), ((), ())), preferred_element_type=jnp.float32
-    ) * model_width ** (-0.5)
-    grad_in = scatter_rows(grad_in.astype(jnp.bfloat16))
-
-    gradients = jnp.stack((grad_in, grad_out), axis=1).astype(jnp.float32)
+    gradients = scatter_rows(jnp.stack((grad_in, grad_out), axis=1).astype(jnp.bfloat16))
     new_moment = beta_one * first_moment[0] + (1.0 - beta_one) * gradients
     new_second = beta_two * second_moment[0] + (1.0 - beta_two) * gradients * gradients
     update = new_moment / correction_one / (jnp.sqrt(new_second / correction_two) + adam_eps)

time: 428 us -> 429 us (level)
  waiting for transfers between devices: 293 us -> 312 us
  starting transfers between devices: 19.4 us -> 8.43 us
  other arithmetic: 35.2 us -> 27.5 us
    ppermute x8 -> x4, waiting for transfers between devices: 25.7 us -> 74.1 us  [swap(): return lax.ppermute(block, name, perm=[(0, 1), (1, 0)])]
    reduce_scatter x4 -> x1, waiting for transfers between devices: 105 us -> 69 us  [scatter_rows(): lax.psum_scatter(block.astype(jnp.bfloat16), 'fx', scatter_dimension=0, t...]
    ppermute x8 -> x4, starting transfers between devices: 18.4 us -> 7.85 us  [swap(): return lax.ppermute(block, name, perm=[(0, 1), (1, 0)])]
    concatenate x2 -> x1, other arithmetic: 8 us -> 1.27 us  [gather_rows(): block = jnp.concatenate([block, swap(block, 'fz')], axis=0)]
    concatenate x0 -> x1, local copies, waits for them, and re-layouts: none -> 6.04 us  [gather_rows(): return jnp.concatenate([block, swap(block, 'fc')], axis=0)]
    slice x3 -> x0, local copies, waits for them, and re-layouts: 4.85 us -> none  [the longest x2 3.84 us: scatter_rows(): own = lax.psum_scatter(block[:half], 'fx', scatter_dimension=0, tiled=True)]
    reduce_scatter x1, waiting for transfers between devices: 27.2 us -> 31.8 us  [group_sum(): flat = lax.psum_scatter(flat, 'gy', scatter_dimension=0, tiled=True)]
    all_gather x4 -> x1, waiting for transfers between devices: 76.3 us -> 79.4 us  [gather_rows(): block = lax.all_gather(block, 'fx', axis=0, tiled=True)]
  transfers between devices with their start and end apart: 20 -> 10, of which waited for: 14 -> 9; matrix products, arithmetic and copies ran while one was open for 14% -> 8% of each run, Pallas kernels for 0% -> 0%
where the time goes in v4:
time: 429 us; the launch traced here: 424 us
  waiting for transfers between devices  312 us (73%)
  local copies, waits for them, and re-layouts  42.6 us (10%)
  other arithmetic  27.5 us (6%)
  matrix products  19.9 us (5%)
  between operations  14 us (3%)
  starting transfers between devices  8.43 us (2%)
    all_gather x1, waiting for transfers between devices, gather_rows(): block = lax.all_gather(block, 'fx', axis=0, tiled=True)  79.4 us
    ppermute x4, waiting for transfers between devices, swap(): return lax.ppermute(block, name, perm=[(0, 1), (1, 0)])  74.1 us
    reduce_scatter x1, waiting for transfers between devices, scatter_rows(): lax.psum_scatter(block.astype(jnp.bfloat16), 'fx', scatter_dimension=0, t...  69 us
    reduce_scatter x1, waiting for transfers between devices, group_sum(): flat = lax.psum_scatter(flat, 'gy', scatter_dimension=0, tiled=True)  31.8 us
    ppermute x2, waiting for transfers between devices, exchange_add(): return values + lax.ppermute(values, name, perm=pairs)  30.9 us
    all_gather x1, waiting for transfers between devices, group_sum(): flat = lax.all_gather(flat, 'gy', axis=0, tiled=True)  26.8 us
    gather x4, local copies, waits for them, and re-layouts, per_device(): partner_rows = jnp.take(blocks, mix_partner[0], axis=0)  15.5 us
    unnamed x25, local copies, waits for them, and re-layouts  13.1 us
  transfers between devices with their start and end apart: 10, of which 9 were waited for; matrix products, arithmetic and copies ran while one was open for 8% of the time, Pallas kernels for 0%

profile of v4, /device:TPU:121, one launch (start us, length us, event | category | flops | bytes accessed | tf_op | source)
XLA Modules:
  0.0 424.4 jit_solution(3666397753914592628)
XLA Ops:
  7.2 0.0 all-gather.3.cloned.1.call-start
  7.2 1.2 copy.54
  8.5 4.3 %collective-permute-start = (bf16[80,2,2560]{2,0,1:T(8,128)(2,1)S(1)}, bf16[80,2,2560]{2,0,1:T(8,128)(2,1)S(1)}, u32[]{:S(2)}, u32[]{:S(2)}) collective-permute-start(bf16[80,2,2560]{2,0,1:T(8,128)(2,1)S(1)} %bitcast.61), channel_id=1, source_target_pairs={{0,2},{2,0},{1,3},{3,1},{4,6},{6,4},{5,7},{7,5},{8,10},{10,8},{9,1... | collective-permute-start | bytes 2457608 | tf_op jit(solution)/shard_map/ppermute | solution.py:50
  12.8 29.5 %collective-permute-done = bf16[80,2,2560]{2,0,1:T(8,128)(2,1)S(1)} collective-permute-done((bf16[80,2,2560]{2,0,1:T(8,128)(2,1)S(1)}, bf16[80,2,2560]{2,0,1:T(8,128)(2,1)S(1)}, u32[]{:S(2)}, u32[]{:S(2)}) %collective-permute-start) | collective-permute-done | bytes 819232 | tf_op jit(solution)/shard_map/ppermute | solution.py:50
  42.2 1.3 pad_maximum_fusion.1
  43.5 0.0 all-gather.3.cloned.1.call-update
  43.5 0.0 reduce-scatter.3.cloned.1.call-start
  43.6 79.4 %all-gather.3.cloned.1.call-done = bf16[640,2,2560]{2,0,1:T(8,128)(2,1)} async-done(((bf16[160,2,2560]{2,0,1:T(8,128)(2,1)}), bf16[640,2,2560]{2,0,1:T(8,128)(2,1)}) %all-gather.3.cloned.1.call-update) | async-done | bytes 6553616 | tf_op jit(solution)/shard_map/all_gather | solution.py:55
  123.0 0.7 collective-permute-start.1
  123.6 0.6 copy.28
  124.3 1.8 copy.29
  126.1 1.9 convert_element_type.72
  128.0 1.6 copy.33
  129.6 4.0 gather_fusion
  133.6 4.1 copy.30
  137.7 3.3 copy.31
  141.1 4.1 gather.9
  145.2 0.1 broadcast_bitcast_fusion
  145.2 0.1 fusion.21
  145.3 2.4 fusion.19
  147.7 0.6 multiply_reduce_fusion
  148.4 0.1 broadcast_multiply_fusion.1
  148.5 1.0 copy-done.1
  149.4 0.8 copy-done.2
  150.2 0.7 multiply_convert_fusion.3
  151.0 0.6 reverse_select_fusion.1
  151.6 0.3 fusion.16
  151.9 0.1 copy.32
  152.1 0.3 fusion.17
  152.4 0.1 copy.34
  152.5 0.7 slice-done
  153.2 0.9 slice-done.1
  154.1 3.1 constant_dynamic-update-slice_fusion.1
  157.2 6.0 %constant_dynamic-update-slice_fusion = bf16[1280,2,2560]{2,0,1:T(8,128)(2,1)} fusion(bf16[1280,2,2560]{2,0,1:T(8,128)(2,1)} %constant_dynamic-update-slice_fusion.1, bf16[640,2,2560]{2,0,1:T(8,128)(2,1)} %collective-permute-done.1), kind=kLoop, calls=%fused_computation.53 | loop fusion | bytes 13107200 | tf_op jit(solution)/shard_map/concatenate | solution.py:56
  163.3 6.0 %fusion.5 = f32[512,2560]{1,0:T(8,128)S(1)} fusion(bf16[512,1280]{0,1:T(8,128)(2,1)S(1)} %bitcast.63, bf16[1280,2,2560]{2,0,1:T(8,128)(2,1)} %constant_dynamic-update-slice_fusion), kind=kOutput, calls=%fused_computation.13 | convolution fusion | flops 3355443200 | bytes 13107200 | tf_op jit(solution)/shard_map/dot_general | solution.py:114
  169.3 0.7 copy-done.4
  169.9 5.9 %multiply_convert_fusion.1 = bf16[512,2560]{1,0:T(8,128)(2,1)S(1)} fusion(f32[512,2560]{1,0:T(8,128)S(1)} %fusion.5, bf16[512,1280]{0,1:T(8,128)(2,1)S(1)} %bitcast.65, bf16[1280,2,2560]{2,0,1:T(8,128)(2,1)S(1)} %copy-done.4), kind=kOutput, calls=%fused_computation.17 | convolution fusion | flops 3371171840 | bytes 15728640 | tf_op jit(solution)/shard_map/dot_general | solution.py:115
  175.9 4.0 fusion.2
  179.8 4.0 fusion.3
  183.8 3.1 pad_maximum_fusion
  187.0 0.0 collective-permute-start.2
  187.0 10.7 %collective-permute-done.2 = bf16[640,2,2560]{2,0,1:T(8,128)(2,1)S(1)} collective-permute-done((bf16[640,2,2560]{2,0,1:T(8,128)(2,1)}, bf16[640,2,2560]{2,0,1:T(8,128)(2,1)S(1)}, u32[]{:S(2)}, u32[]{:S(2)}) %collective-permute-start.2) | collective-permute-done | bytes 6553632 | tf_op jit(solution)/shard_map/ppermute | solution.py:50
  197.7 3.9 add_convert_fusion
  201.6 0.0 reduce-scatter.5.cloned.1.call-start
  201.7 69.0 %reduce-scatter.3.cloned.1.call-done = bf16[160,2,2560]{2,0,1:T(8,128)(2,1)} async-done(((bf16[640,2,2560]{2,0,1:T(8,128)(2,1)}), bf16[160,2,2560]{2,0,1:T(8,128)(2,1)}) %reduce-scatter.3.cloned.1.call-update) | async-done | bytes 1638416 | tf_op jit(solution)/shard_map/reduce_scatter | solution.py:62
  270.7 1.2 slice.31
  271.9 2.9 collective-permute-start.3
  274.8 33.9 %collective-permute-done.3 = bf16[80,2,2560]{2,0,1:T(8,128)(2,1)S(1)} collective-permute-done((bf16[80,2,2560]{2,0,1:T(8,128)(2,1)S(1)}, bf16[80,2,2560]{2,0,1:T(8,128)(2,1)S(1)}, u32[]{:S(2)}, u32[]{:S(2)}) %collective-permute-start.3) | collective-permute-done | bytes 819232 | tf_op jit(solution)/shard_map/ppermute | solution.py:50
  308.7 4.0 fusion.10
  312.7 1.3 copy.38
  314.0 2.5 reshape.152
  316.5 0.0 all-gather.5.cloned.1.call-start
  316.5 31.8 %reduce-scatter.5.cloned.1.call-done = f32[800,128]{1,0:T(8,128)} async-done(((f32[3200,128]{1,0:T(8,128)}), f32[800,128]{1,0:T(8,128)}) %reduce-scatter.5.cloned.1.call-update) | async-done | bytes 409616 | tf_op jit(solution)/shard_map/reduce_scatter | solution.py:76
  348.3 0.2 collective-permute-start.4
  348.5 10.0 %collective-permute-done.4 = f32[800,128]{1,0:T(8,128)S(1)} collective-permute-done((f32[800,128]{1,0:T(8,128)}, f32[800,128]{1,0:T(8,128)S(1)}, u32[]{:S(2)}, u32[]{:S(2)}) %collective-permute-start.4) | collective-permute-done | bytes 409632 | tf_op jit(solution)/shard_map/ppermute | solution.py:69
  358.5 1.1 add.96
  359.5 0.2 collective-permute-start.5
  359.8 20.8 %collective-permute-done.5 = f32[800,128]{1,0:T(8,128)S(1)} collective-permute-done((f32[800,128]{1,0:T(8,128)S(1)}, f32[800,128]{1,0:T(8,128)S(1)}, u32[]{:S(2)}, u32[]{:S(2)}) %collective-permute-start.5) | collective-permute-done | bytes 409632 | tf_op jit(solution)/shard_map/ppermute | solution.py:69
  380.6 0.8 add.97
  381.4 2.4 copy.39
  383.9 26.8 %all-gather.5.cloned.1.call-done = f32[3200,128]{1,0:T(8,128)} async-done(((f32[800,128]{1,0:T(8,128)}), f32[3200,128]{1,0:T(8,128)}) %all-gather.5.cloned.1.call-update) | async-done | bytes 1638416 | tf_op jit(solution)/shard_map/all_gather | solution.py:81
  410.6 1.5 broadcast_multiply_fusion
  412.1 0.9 mul.206
  413.0 4.8 %multiply_subtract_fusion = (f32[80,2,2560]{2,1,0:T(2,128)}, f32[80,2,2560]{2,1,0:T(2,128)}) fusion(f32[80,2,2560]{2,1,0:T(2,128)} %param.16, f32[80,2,2560]{2,1,0:T(2,128)S(1)} %mul.206, f32[80,2,2560]{2,1,0:T(2,128)} %param.17), kind=kLoop, calls=%fused_computation.42 | loop fusion | flops 2457600 | bytes 8192000 | tf_op jit(solution)/shard_map/sub | solution.py:138
  (25 shorter events, 0.1 us)
Async XLA Ops:
  7.2 115.8 %all-gather.3.cloned.1.call-start = ((), (), s32[]{:S(2)}) async-start(), calls=%async_computation.2 | async-start | bytes 8192000 | tf_op jit(solution)/shard_map/all_gather | solution.py:55
  8.4 115.2 %copy-start.5 = (bf16[1,512,1280]{2,1,0:T(8,128)(2,1)S(1)}, bf16[1,512,1280]{2,1,0:T(8,128)(2,1)}, u32[]{:S(2)}) copy-start(bf16[1,512,1280]{2,1,0:T(8,128)(2,1)} %param.9) | copy-start | bytes 3932164
  8.5 33.8 %collective-permute-start = (bf16[80,2,2560]{2,0,1:T(8,128)(2,1)S(1)}, bf16[80,2,2560]{2,0,1:T(8,128)(2,1)S(1)}, u32[]{:S(2)}, u32[]{:S(2)}) collective-permute-start(bf16[80,2,2560]{2,0,1:T(8,128)(2,1)S(1)} %bitcast.61), channel_id=1, source_target_pairs={{0,2},{2,0},{1,3},{3,1},{4,6},{6,4},{5,7},{7,5},{8,10},{10,8},{9,1... | collective-permute-start | bytes 2457608 | tf_op jit(solution)/shard_map/ppermute | solution.py:50
  43.5 227.2 %reduce-scatter.3.cloned.1.call-start = ((), (), s32[]{:S(2)}) async-start(), calls=%async_computation.3 | async-start | bytes 8192000 | tf_op jit(solution)/shard_map/reduce_scatter | solution.py:62
  123.0 34.3 %collective-permute-start.1 = (bf16[640,2,2560]{2,0,1:T(8,128)(2,1)}, bf16[640,2,2560]{2,0,1:T(8,128)(2,1)}, u32[]{:S(2)}, u32[]{:S(2)}) collective-permute-start(bf16[640,2,2560]{2,0,1:T(8,128)(2,1)} %all-gather.3.cloned.1.call-done), channel_id=1, source_target_pairs={{0,1},{1,0},{2,3},{3,2},{4,5},{5,4},{6,7},{7,6},{8,9},{9,8},{10,11... | collective-permute-start | bytes 19660808 | tf_op jit(solution)/shard_map/ppermute | solution.py:50
  126.1 3.5 copy-start.6
  141.0 4.2 copy-start.7
  145.2 2.5 copy-start
  147.7 1.7 copy-start.1
  147.7 2.5 copy-start.2
  151.0 2.2 slice-start
  151.6 2.5 slice-start.1
  163.3 6.6 %copy-start.4 = (bf16[1280,2,2560]{2,0,1:T(8,128)(2,1)S(1)}, bf16[1280,2,2560]{2,0,1:T(8,128)(2,1)}, u32[]{:S(2)}) copy-start(bf16[1280,2,2560]{2,0,1:T(8,128)(2,1)} %constant_dynamic-update-slice_fusion) | copy-start | bytes 39321604
  187.0 10.7 %collective-permute-start.2 = (bf16[640,2,2560]{2,0,1:T(8,128)(2,1)}, bf16[640,2,2560]{2,0,1:T(8,128)(2,1)S(1)}, u32[]{:S(2)}, u32[]{:S(2)}) collective-permute-start(bf16[640,2,2560]{2,0,1:T(8,128)(2,1)} %pad_maximum_fusion), channel_id=1, source_target_pairs={{0,1},{1,0},{2,3},{3,2},{4,5},{5,4},{6,7},{7,6},{8,9},{9,8},{10,11... | collective-permute-start | bytes 19660808 | tf_op jit(solution)/shard_map/ppermute | solution.py:50
  201.6 107.1 %copy-start.3 = (f32[80,2,2560]{2,1,0:T(2,128)S(1)}, f32[80,2,2560]{2,1,0:T(2,128)}, u32[]{:S(2)}) copy-start(f32[80,2,2560]{2,1,0:T(2,128)} %param.16) | copy-start | bytes 4915204
  201.6 146.7 %reduce-scatter.5.cloned.1.call-start = ((), (), s32[]{:S(2)}) async-start(), calls=%async_computation.4 | async-start | bytes 2048000 | tf_op jit(solution)/shard_map/reduce_scatter | solution.py:76
  271.9 36.8 %collective-permute-start.3 = (bf16[80,2,2560]{2,0,1:T(8,128)(2,1)S(1)}, bf16[80,2,2560]{2,0,1:T(8,128)(2,1)S(1)}, u32[]{:S(2)}, u32[]{:S(2)}) collective-permute-start(bf16[80,2,2560]{2,0,1:T(8,128)(2,1)S(1)} %slice.31), channel_id=1, source_target_pairs={{0,2},{2,0},{1,3},{3,1},{4,6},{6,4},{5,7},{7,5},{8,10},{10,8},{9,1... | collective-permute-start | bytes 2457608 | tf_op jit(solution)/shard_map/ppermute | solution.py:50
  316.5 94.2 %all-gather.5.cloned.1.call-start = ((), (), s32[]{:S(2)}) async-start(), calls=%async_computation.5 | async-start | bytes 2048000 | tf_op jit(solution)/shard_map/all_gather | solution.py:81
  348.3 10.2 %collective-permute-start.4 = (f32[800,128]{1,0:T(8,128)}, f32[800,128]{1,0:T(8,128)S(1)}, u32[]{:S(2)}, u32[]{:S(2)}) collective-permute-start(f32[800,128]{1,0:T(8,128)} %reduce-scatter.5.cloned.1.call-done), channel_id=1, source_target_pairs={{0,64},{64,0},{128,192},{192,128},{1,65},{65,1},{129,193},{193,129... | collective-permute-start | bytes 1228808 | tf_op jit(solution)/shard_map/ppermute | solution.py:69
  359.5 21.1 %collective-permute-start.5 = (f32[800,128]{1,0:T(8,128)S(1)}, f32[800,128]{1,0:T(8,128)S(1)}, u32[]{:S(2)}, u32[]{:S(2)}) collective-permute-start(f32[800,128]{1,0:T(8,128)S(1)} %add.96), channel_id=1, source_target_pairs={{0,128},{64,192},{128,0},{192,64},{1,129},{65,193},{129,1},{193,65... | collective-permute-start | bytes 1228808 | tf_op jit(solution)/shard_map/ppermute | solution.py:69
Sparse Core Ops, SparseCore 0:
  43.6 79.2 all-gather.2
  201.7 68.9 reduce-scatter.2
  316.6 31.6 reduce-scatter.4
  381.5 29.0 all-gather.4

commit v5 on v4

--- a/solution.py
+++ b/solution.py
@@ -43,25 +43,31 @@
     split = columns.reshape(rows, sizes["fx"], sizes["fz"], sizes["fc"], local)
     split = jnp.where(lax.axis_index("fz") == 0, split, jnp.flip(split, axis=2))
     split = jnp.where(lax.axis_index("fc") == 0, split, jnp.flip(split, axis=3))
-    return jnp.transpose(split, (0, 3, 1, 2, 4)).reshape(columns.shape)
+    return jnp.transpose(split, (0, 3, 2, 1, 4)).reshape(columns.shape)
 
 
 def swap(block, name):
     return lax.ppermute(block, name, perm=[(0, 1), (1, 0)])
 
 
-def gather_rows(block):
-    block = jnp.concatenate([block, swap(block, "fz")], axis=0)
-    block = lax.all_gather(block, "fx", axis=0, tiled=True)
-    return jnp.concatenate([block, swap(block, "fc")], axis=0)
+def gather_rows(block, prologue):
+    own = lax.all_gather(block, "fx", axis=0, tiled=True)
+    partner, prologue = lax.optimization_barrier((swap(block, "fz"), prologue))
+    partner = lax.all_gather(partner, "fx", axis=0, tiled=True)
+    block = jnp.concatenate([own, partner], axis=0)
+    return jnp.concatenate([block, swap(block, "fc")], axis=0), prologue
 
 
 def scatter_rows(block):
     half = block.shape[0] // 2
     block = block[:half].astype(jnp.float32) + swap(block[half:], "fc").astype(jnp.float32)
-    block = lax.psum_scatter(block.astype(jnp.bfloat16), "fx", scatter_dimension=0, tiled=True)
+    block = block.astype(jnp.bfloat16)
     half = block.shape[0] // 2
-    return block[:half].astype(jnp.float32) + swap(block[half:], "fz").astype(jnp.float32)
+    partner = lax.psum_scatter(block[half:], "fx", scatter_dimension=0, tiled=True)
+    own, partner = lax.optimization_barrier((block[:half], partner))
+    partner = swap(partner, "fz")
+    own = lax.psum_scatter(own, "fx", scatter_dimension=0, tiled=True)
+    return own.astype(jnp.float32) + partner.astype(jnp.float32)
 
 
 def exchange_add(values, name, size, stride):
@@ -105,10 +111,8 @@
     offsets = lax.broadcasted_iota(jnp.int32, (utt_count, crop_frames), 1)
     keep_mask = (offsets < lengths[0][:, None]).reshape(frame_rows, 1).astype(jnp.bfloat16)
     masked_grad = cotangent[0] * keep_mask
-    normed = gathered_order(normed)
-    masked_grad = gathered_order(masked_grad)
-
-    weights = gather_rows(inner_params[0])
+    prologue = (gathered_order(normed), gathered_order(masked_grad))
+    weights, (normed, masked_grad) = gather_rows(inner_params[0], prologue)
     w_in = weights[:, 0, :]
     w_out = weights[:, 1, :]
     pre_act = jnp.dot(normed, w_in, preferred_element_type=jnp.float32) * model_width ** (-0.5)

time: 429 us -> 378 us (0.88)
  waiting for transfers between devices: 312 us -> 244 us
  other arithmetic: 27.5 us -> 50 us
    all_gather x1 -> x2, waiting for transfers between devices: 79.4 us -> 56.5 us  [the longest x1 45.8 us: gather_rows(): partner = lax.all_gather(partner, 'fx', axis=0, tiled=True)]
    concatenate x1 -> x2, other arithmetic: 1.27 us -> 23.4 us  [the longest x1 17.1 us: gather_rows(): return (jnp.concatenate([block, swap(block, 'fc')], axis=0), prologue)]
    reduce_scatter x1 -> x2, waiting for transfers between devices: 69 us -> 48.1 us  [the longest x1 41.9 us: scatter_rows(): lax.psum_scatter(block[half:], 'fx', scatter_dimension=0, tiled=True)]
    ppermute x4, waiting for transfers between devices: 74.1 us -> 55.3 us  [swap(): return lax.ppermute(block, name, perm=[(0, 1), (1, 0)])]
    concatenate x1 -> x0, local copies, waits for them, and re-layouts: 6.04 us -> none  [gather_rows(): return jnp.concatenate([block, swap(block, 'fc')], axis=0)]
    reduce_scatter x1, waiting for transfers between devices: 31.8 us -> 26.8 us  [group_sum(): flat = lax.psum_scatter(flat, 'gy', scatter_dimension=0, tiled=True)]
    slice x1, local copies, waits for them, and re-layouts: 1.2 us -> 6 us  [scatter_rows(): block[half:]]
    unnamed x25 -> x26, local copies, waits for them, and re-layouts: 13.1 us -> 10.7 us
  transfers between devices with their start and end apart: 10 -> 12, of which waited for: 9 -> 12; matrix products, arithmetic and copies ran while one was open for 8% -> 8% of each run, Pallas kernels for 0% -> 0%
where the time goes in v5:
time: 378 us; the launch traced here: 374 us
  waiting for transfers between devices  244 us (65%)
  other arithmetic  50 us (13%)
  local copies, waits for them, and re-layouts  39.3 us (10%)
  matrix products  17.5 us (5%)
  between operations  14.3 us (4%)
  starting transfers between devices  8.77 us (2%)
    ppermute x4, waiting for transfers between devices, swap(): return lax.ppermute(block, name, perm=[(0, 1), (1, 0)])  55.3 us
    all_gather x1, waiting for transfers between devices, gather_rows(): partner = lax.all_gather(partner, 'fx', axis=0, tiled=True)  45.8 us
    reduce_scatter x1, waiting for transfers between devices, scatter_rows(): lax.psum_scatter(block[half:], 'fx', scatter_dimension=0, tiled=True)  41.9 us
    ppermute x2, waiting for transfers between devices, exchange_add(): return values + lax.ppermute(values, name, perm=pairs)  30.9 us
    reduce_scatter x1, waiting for transfers between devices, group_sum(): flat = lax.psum_scatter(flat, 'gy', scatter_dimension=0, tiled=True)  26.8 us
    all_gather x1, waiting for transfers between devices, group_sum(): flat = lax.all_gather(flat, 'gy', axis=0, tiled=True)  26.7 us
    concatenate x1, other arithmetic, gather_rows(): return (jnp.concatenate([block, swap(block, 'fc')], axis=0), prologue)  17.1 us
    gather x4, local copies, waits for them, and re-layouts, per_device(): partner_rows = jnp.take(blocks, mix_partner[0], axis=0)  15.8 us
  transfers between devices with their start and end apart: 12, of which 12 were waited for; matrix products, arithmetic and copies ran while one was open for 8% of the time, Pallas kernels for 0%

profile of v5, /device:TPU:121, one launch (start us, length us, event | category | flops | bytes accessed | tf_op | source)
XLA Modules:
  0.0 374.1 jit_solution(17728995757189911405)
XLA Ops:
  7.2 2.2 copy.57
  9.5 0.0 all-gather.5.cloned.1.call-start
  9.5 4.3 %collective-permute-start = (bf16[80,2,2560]{2,0,1:T(8,128)(2,1)}, bf16[80,2,2560]{2,0,1:T(8,128)(2,1)S(1)}, u32[]{:S(2)}, u32[]{:S(2)}) collective-permute-start(bf16[80,2,2560]{2,0,1:T(8,128)(2,1)} %bitcast.60), channel_id=1, source_target_pairs={{0,2},{2,0},{1,3},{3,1},{4,6},{6,4},{5,7},{7,5},{8,10},{10,8},{9,1... | collective-permute-start | bytes 2457608 | tf_op jit(solution)/shard_map/ppermute | solution.py:50
  13.8 0.6 copy.31
  14.5 1.9 copy.32
  16.4 1.9 convert_element_type.72
  18.3 1.6 copy.36
  19.9 4.0 %gather_fusion = f32[4,128,1280]{2,1,0:T(8,128)} fusion(f32[4,128,1280]{2,1,0:T(8,128)} %bitcast.58, s32[1024]{0:T(1024)S(1)} %pad_clamp_fusion), kind=kCustom, calls=%fused_computation | custom fusion | bytes 5242896 | tf_op jit(solution)/shard_map/jit(_take)/gather | solution.py:108
  23.9 4.3 %copy.33 = f32[4,128,1280]{1,0,2:T(4,128)} copy(f32[4,128,1280]{2,1,0:T(8,128)} %gather_fusion) | data formatting | bytes 5242880 | tf_op jit(solution)/shard_map/jit(_take)/gather | solution.py:108
  28.2 3.3 copy.34
  31.5 4.2 %gather.9 = f32[512,4,2,2,80]{0,4,3,2,1:T(8,128)} reshape(f32[4,128,1280]{1,0,2:T(4,128)} %copy.33) | data formatting | bytes 5242880 | tf_op jit(solution)/shard_map/jit(_take)/gather | solution.py:108
  35.7 0.1 broadcast_bitcast_fusion
  35.8 0.1 fusion.21
  35.9 2.4 fusion.19
  38.3 0.6 multiply_reduce_fusion
  38.9 0.1 broadcast_multiply_fusion.1
  39.0 1.0 copy-done.3
  40.1 0.8 copy-done.4
  40.8 0.7 multiply_convert_fusion.3
  41.6 0.7 reverse_select_fusion.1
  42.3 0.3 fusion.16
  42.6 0.1 copy.35
  42.7 0.3 fusion.17
  43.0 0.1 copy.37
  43.1 0.5 collective-permute-done
  43.6 0.9 copy-done.7
  44.5 0.0 reduce-scatter.4.cloned.1.call-start
  44.5 10.7 %all-gather.9.cloned.1.call-done = bf16[1,320,2,2560]{3,1,2,0:T(8,128)(2,1)} async-done(((bf16[1,80,2,2560]{3,1,2,0:T(8,128)(2,1)}), bf16[1,320,2,2560]{3,1,2,0:T(8,128)(2,1)}) %all-gather.9.cloned.1.call-update) | async-done | bytes 3276816 | tf_op jit(solution)/shard_map/all_gather | solution.py:54
  55.2 45.8 %all-gather.5.cloned.1.call-done = bf16[320,2,2560]{2,0,1:T(8,128)(2,1)} async-done(((bf16[80,2,2560]{2,0,1:T(8,128)(2,1)}), bf16[320,2,2560]{2,0,1:T(8,128)(2,1)}) %all-gather.5.cloned.1.call-update) | async-done | bytes 3276816 | tf_op jit(solution)/shard_map/all_gather | solution.py:56
  101.0 6.3 %pad_maximum_fusion.2 = bf16[640,2,2560]{2,0,1:T(8,128)(2,1)} fusion(bf16[320,2,2560]{2,0,1:T(8,128)(2,1)} %all-gather.5.cloned.1.call-done, bf16[320,2,2560]{2,0,1:T(8,128)(2,1)} %bitcast.55), kind=kLoop, calls=%fused_computation.17 | loop fusion | flops 13107200 | bytes 13107200 | tf_op jit(solution)/shard_map/concatenate | solution.py:57
  107.3 0.7 collective-permute-start.1
  108.0 10.4 %collective-permute-done.1 = bf16[640,2,2560]{2,0,1:T(8,128)(2,1)S(1)} collective-permute-done((bf16[640,2,2560]{2,0,1:T(8,128)(2,1)}, bf16[640,2,2560]{2,0,1:T(8,128)(2,1)S(1)}, u32[]{:S(2)}, u32[]{:S(2)}) %collective-permute-start.1) | collective-permute-done | bytes 6553632 | tf_op jit(solution)/shard_map/ppermute | solution.py:50
  118.3 17.1 %pad_maximum_fusion = bf16[1280,2,2560]{2,0,1:T(8,128)(2,1)S(1)} fusion(bf16[640,2,2560]{2,0,1:T(8,128)(2,1)S(1)} %collective-permute-done.1, bf16[320,2,2560]{2,0,1:T(8,128)(2,1)S(1)} %copy-done.2, bf16[320,2,2560]{2,0,1:T(8,128)(2,1)S(1)} %bitcast.56), kind=kLoop, calls=%fused_computation.3 | loop fusion | flops 39321600 | bytes 26214400 | tf_op jit(solution)/shard_map/concatenate | solution.py:58
  135.5 3.7 fusion.5
  139.2 6.0 %multiply_convert_fusion.1 = bf16[512,2560]{1,0:T(8,128)(2,1)S(1)} fusion(f32[512,2560]{1,0:T(8,128)S(1)} %fusion.5, bf16[512,1280]{0,1:T(8,128)(2,1)S(1)} %bitcast.63, bf16[1280,2,2560]{2,0,1:T(8,128)(2,1)S(1)} %pad_maximum_fusion), kind=kOutput, calls=%fused_computation.19 | convolution fusion | flops 3371171840 | bytes 15728640 | tf_op jit(solution)/shard_map/dot_general | solution.py:119
  145.2 4.0 %fusion.2 = bf16[1280,1,2560]{2,0,1:T(8,128)(2,1)S(1)} fusion(bf16[512,1280]{0,1:T(8,128)(2,1)S(1)} %bitcast.64, f32[512,2560]{1,0:T(8,128)S(1)} %fusion.5), kind=kOutput, calls=%fused_computation.9 | convolution fusion | flops 3369861120 | bytes 13107200 | tf_op jit(solution)/shard_map/dot_general | solution.py:126
  149.2 3.8 %fusion.3 = bf16[1280,1,2560]{2,0,1:T(8,128)(2,1)S(1)} fusion(bf16[512,1280]{0,1:T(8,128)(2,1)S(1)} %bitcast.62, bf16[512,2560]{1,0:T(8,128)(2,1)S(1)} %multiply_convert_fusion.1), kind=kOutput, calls=%fused_computation.10 | convolution fusion | flops 3361996800 | bytes 10485760 | tf_op jit(solution)/shard_map/dot_general | solution.py:123
  153.0 3.1 pad_maximum_fusion.1
  156.1 0.4 collective-permute-start.2
  156.5 10.4 %collective-permute-done.2 = bf16[640,2,2560]{2,0,1:T(8,128)(2,1)S(1)} collective-permute-done((bf16[640,2,2560]{2,0,1:T(8,128)(2,1)}, bf16[640,2,2560]{2,0,1:T(8,128)(2,1)S(1)}, u32[]{:S(2)}, u32[]{:S(2)}) %collective-permute-start.2) | collective-permute-done | bytes 6553632 | tf_op jit(solution)/shard_map/ppermute | solution.py:50
  166.9 3.8 %add_convert_fusion = bf16[640,2,2560]{2,0,1:T(8,128)(2,1)} fusion(bf16[640,2,2560]{2,0,1:T(8,128)(2,1)S(1)} %collective-permute-done.2, bf16[1280,1,2560]{2,0,1:T(8,128)(2,1)S(1)} %fusion.3, bf16[1280,1,2560]{2,0,1:T(8,128)(2,1)S(1)} %fusion.2), kind=kLoop, calls=%fused_computation.6 | loop fusion | flops 16384000 | bytes 26214400 | tf_op jit(solution)/shard_map/convert_element_type | solution.py:64
  170.7 6.0 %fusion.24 = (bf16[320,2,2560]{2,0,1:T(8,128)(2,1)}, bf16[320,2,2560]{2,0,1:T(8,128)(2,1)}) fusion(bf16[640,2,2560]{2,0,1:T(8,128)(2,1)} %add_convert_fusion), kind=kLoop, calls=%fused_computation.65 | loop fusion | bytes 13107200 | tf_op jit(solution)/shard_map/slice | solution.py:66
  176.7 0.0 reduce-scatter.6.cloned.1.call-start
  176.8 41.9 %reduce-scatter.4.cloned.1.call-done = bf16[80,2,2560]{2,0,1:T(8,128)(2,1)} async-done(((bf16[320,2,2560]{2,0,1:T(8,128)(2,1)}), bf16[80,2,2560]{2,0,1:T(8,128)(2,1)}) %reduce-scatter.4.cloned.1.call-update) | async-done | bytes 819216 | tf_op jit(solution)/shard_map/reduce_scatter | solution.py:66
  218.8 1.1 copy-done.8
  219.9 2.8 collective-permute-start.3
  222.6 34.0 %collective-permute-done.3 = bf16[80,2,2560]{2,0,1:T(8,128)(2,1)} collective-permute-done((bf16[80,2,2560]{2,0,1:T(8,128)(2,1)S(1)}, bf16[80,2,2560]{2,0,1:T(8,128)(2,1)}, u32[]{:S(2)}, u32[]{:S(2)}) %collective-permute-start.3) | collective-permute-done | bytes 819232 | tf_op jit(solution)/shard_map/ppermute | solution.py:50
  256.7 6.1 %reduce-scatter.6.cloned.1.call-done = bf16[80,2,2560]{2,0,1:T(8,128)(2,1)} async-done(((bf16[320,2,2560]{2,0,1:T(8,128)(2,1)}), bf16[80,2,2560]{2,0,1:T(8,128)(2,1)}) %reduce-scatter.6.cloned.1.call-update) | async-done | bytes 819216 | tf_op jit(solution)/shard_map/reduce_scatter | solution.py:69
  262.8 4.2 %fusion.10 = (f32[80,2,2560]{2,0,1:T(8,128)S(1)}, f32[1,80,2,2560]{3,1,2,0:T(8,128)S(1)}) fusion(f32[80,2,2560]{2,1,0:T(2,128)S(1)} %copy-done.5, f32[1,80,2,2560]{3,2,1,0:T(2,128)} %param.15, bf16[80,2,2560]{2,0,1:T(8,128)(2,1)} %collective-permute-done.3, bf16[80,2,2560]{2,0,1:T(8,128)(2,1)} %reduce-scatter.6.cloned.1.call-done, ...), kind=kLoop, calls=%fused_computation.34 | loop fusion | flops 7782400 | bytes 10649600 | tf_op jit(solution)/shard_map/sub | solution.py:135
  267.1 1.3 copy.41
  268.3 2.5 reshape.152
  270.8 0.0 all-gather.7.cloned.1.call-start
  270.9 26.8 %reduce-scatter.8.cloned.1.call-done = f32[800,128]{1,0:T(8,128)} async-done(((f32[3200,128]{1,0:T(8,128)}), f32[800,128]{1,0:T(8,128)}) %reduce-scatter.8.cloned.1.call-update) | async-done | bytes 409616 | tf_op jit(solution)/shard_map/reduce_scatter | solution.py:82
  297.7 0.2 collective-permute-start.4
  297.9 10.0 %collective-permute-done.4 = f32[800,128]{1,0:T(8,128)S(1)} collective-permute-done((f32[800,128]{1,0:T(8,128)}, f32[800,128]{1,0:T(8,128)S(1)}, u32[]{:S(2)}, u32[]{:S(2)}) %collective-permute-start.4) | collective-permute-done | bytes 409632 | tf_op jit(solution)/shard_map/ppermute | solution.py:75
  307.9 1.1 add.98
  309.0 0.2 collective-permute-start.5
  309.2 20.9 %collective-permute-done.5 = f32[800,128]{1,0:T(8,128)S(1)} collective-permute-done((f32[800,128]{1,0:T(8,128)S(1)}, f32[800,128]{1,0:T(8,128)S(1)}, u32[]{:S(2)}, u32[]{:S(2)}) %collective-permute-start.5) | collective-permute-done | bytes 409632 | tf_op jit(solution)/shard_map/ppermute | solution.py:75
  330.0 0.8 add.99
  330.9 2.4 copy.42
  333.3 26.7 %all-gather.7.cloned.1.call-done = f32[3200,128]{1,0:T(8,128)} async-done(((f32[800,128]{1,0:T(8,128)}), f32[3200,128]{1,0:T(8,128)}) %all-gather.7.cloned.1.call-update) | async-done | bytes 1638416 | tf_op jit(solution)/shard_map/all_gather | solution.py:87
  360.0 1.5 broadcast_multiply_fusion
  361.5 0.9 mul.206
  362.4 4.8 %multiply_subtract_fusion = (f32[80,2,2560]{2,1,0:T(2,128)}, f32[80,2,2560]{2,1,0:T(2,128)}) fusion(f32[80,2,2560]{2,1,0:T(2,128)} %param.16, f32[80,2,2560]{2,1,0:T(2,128)S(1)} %mul.206, f32[80,2,2560]{2,1,0:T(2,128)} %param.17), kind=kLoop, calls=%fused_computation.43 | loop fusion | flops 2457600 | bytes 8192000 | tf_op jit(solution)/shard_map/sub | solution.py:142
  (31 shorter events, 0.2 us)
Async XLA Ops:
  7.2 6.6 %copy-start.6 = (bf16[1,512,1280]{2,1,0:T(8,128)(2,1)S(1)}, bf16[1,512,1280]{2,1,0:T(8,128)(2,1)}, u32[]{:S(2)}) copy-start(bf16[1,512,1280]{2,1,0:T(8,128)(2,1)} %param.9) | copy-start | bytes 3932164
  7.2 48.0 %all-gather.9.cloned.1.call-start = ((), (), s32[]{:S(2)}) async-start(), calls=%async_computation.8 | async-start | bytes 4096000 | tf_op jit(solution)/shard_map/all_gather | solution.py:54
  9.5 91.6 %all-gather.5.cloned.1.call-start = ((), (), s32[]{:S(2)}) async-start(), calls=%async_computation.3 | async-start | bytes 4096000 | tf_op jit(solution)/shard_map/all_gather | solution.py:56
  9.5 34.1 %collective-permute-start = (bf16[80,2,2560]{2,0,1:T(8,128)(2,1)}, bf16[80,2,2560]{2,0,1:T(8,128)(2,1)S(1)}, u32[]{:S(2)}, u32[]{:S(2)}) collective-permute-start(bf16[80,2,2560]{2,0,1:T(8,128)(2,1)} %bitcast.60), channel_id=1, source_target_pairs={{0,2},{2,0},{1,3},{3,1},{4,6},{6,4},{5,7},{7,5},{8,10},{10,8},{9,1... | collective-permute-start | bytes 2457608 | tf_op jit(solution)/shard_map/ppermute | solution.py:50
  16.4 3.5 copy-start.9
  31.5 4.3 %copy-start.10 = (s32[1,4]{1,0:T(1,128)S(1)}, s32[1,4]{1,0:T(1,128)}, u32[]{:S(2)}) copy-start(s32[1,4]{1,0:T(1,128)} %param.12) | copy-start | bytes 52
  35.7 2.6 copy-start
  38.3 1.8 copy-start.3
  38.3 2.6 copy-start.4
  43.6 0.9 copy-start.7
  44.5 174.2 %reduce-scatter.4.cloned.1.call-start = ((), (), s32[]{:S(2)}) async-start(), calls=%async_computation.4 | async-start | bytes 4096000 | tf_op jit(solution)/shard_map/reduce_scatter | solution.py:66
  101.0 17.3 %copy-start.1 = (bf16[1,320,2,2560]{3,1,2,0:T(8,128)(2,1)S(1)}, bf16[1,320,2,2560]{3,1,2,0:T(8,128)(2,1)}, u32[]{:S(2)}) copy-start(bf16[1,320,2,2560]{3,1,2,0:T(8,128)(2,1)} %all-gather.9.cloned.1.call-done) | copy-start | bytes 9830404
  101.0 17.3 %copy-start.2 = (bf16[320,2,2560]{2,0,1:T(8,128)(2,1)S(1)}, bf16[320,2,2560]{2,0,1:T(8,128)(2,1)}, u32[]{:S(2)}) copy-start(bf16[320,2,2560]{2,0,1:T(8,128)(2,1)} %all-gather.5.cloned.1.call-done) | copy-start | bytes 9830404
  107.3 11.0 %collective-permute-start.1 = (bf16[640,2,2560]{2,0,1:T(8,128)(2,1)}, bf16[640,2,2560]{2,0,1:T(8,128)(2,1)S(1)}, u32[]{:S(2)}, u32[]{:S(2)}) collective-permute-start(bf16[640,2,2560]{2,0,1:T(8,128)(2,1)} %pad_maximum_fusion.2), channel_id=1, source_target_pairs={{0,1},{1,0},{2,3},{3,2},{4,5},{5,4},{6,7},{7,6},{8,9},{9,8},{10,11... | collective-permute-start | bytes 19660808 | tf_op jit(solution)/shard_map/ppermute | solution.py:50
  156.1 10.7 %collective-permute-start.2 = (bf16[640,2,2560]{2,0,1:T(8,128)(2,1)}, bf16[640,2,2560]{2,0,1:T(8,128)(2,1)S(1)}, u32[]{:S(2)}, u32[]{:S(2)}) collective-permute-start(bf16[640,2,2560]{2,0,1:T(8,128)(2,1)} %pad_maximum_fusion.1), channel_id=1, source_target_pairs={{0,1},{1,0},{2,3},{3,2},{4,5},{5,4},{6,7},{7,6},{8,9},{9,8},{10,11... | collective-permute-start | bytes 19660808 | tf_op jit(solution)/shard_map/ppermute | solution.py:50
  176.7 86.1 %copy-start.5 = (f32[80,2,2560]{2,1,0:T(2,128)S(1)}, f32[80,2,2560]{2,1,0:T(2,128)}, u32[]{:S(2)}) copy-start(f32[80,2,2560]{2,1,0:T(2,128)} %param.16) | copy-start | bytes 4915204
  176.7 86.1 %reduce-scatter.6.cloned.1.call-start = ((), (), s32[]{:S(2)}) async-start(), calls=%async_computation.5 | async-start | bytes 4096000 | tf_op jit(solution)/shard_map/reduce_scatter | solution.py:69
  218.7 1.1 copy-start.8
  218.8 78.9 %reduce-scatter.8.cloned.1.call-start = ((), (), s32[]{:S(2)}) async-start(), calls=%async_computation.6 | async-start | bytes 2048000 | tf_op jit(solution)/shard_map/reduce_scatter | solution.py:82
  219.9 36.8 %collective-permute-start.3 = (bf16[80,2,2560]{2,0,1:T(8,128)(2,1)S(1)}, bf16[80,2,2560]{2,0,1:T(8,128)(2,1)}, u32[]{:S(2)}, u32[]{:S(2)}) collective-permute-start(bf16[80,2,2560]{2,0,1:T(8,128)(2,1)S(1)} %copy-done.8), channel_id=1, source_target_pairs={{0,2},{2,0},{1,3},{3,1},{4,6},{6,4},{5,7},{7,5},{8,10},{10,8},{9,1... | collective-permute-start | bytes 2457608 | tf_op jit(solution)/shard_map/ppermute | solution.py:50
  270.8 89.2 %all-gather.7.cloned.1.call-start = ((), (), s32[]{:S(2)}) async-start(), calls=%async_computation.7 | async-start | bytes 2048000 | tf_op jit(solution)/shard_map/all_gather | solution.py:87
  297.7 10.2 %collective-permute-start.4 = (f32[800,128]{1,0:T(8,128)}, f32[800,128]{1,0:T(8,128)S(1)}, u32[]{:S(2)}, u32[]{:S(2)}) collective-permute-start(f32[800,128]{1,0:T(8,128)} %reduce-scatter.8.cloned.1.call-done), channel_id=1, source_target_pairs={{0,64},{64,0},{128,192},{192,128},{1,65},{65,1},{129,193},{193,129... | collective-permute-start | bytes 1228808 | tf_op jit(solution)/shard_map/ppermute | solution.py:75
  309.0 21.1 %collective-permute-start.5 = (f32[800,128]{1,0:T(8,128)S(1)}, f32[800,128]{1,0:T(8,128)S(1)}, u32[]{:S(2)}, u32[]{:S(2)}) collective-permute-start(f32[800,128]{1,0:T(8,128)S(1)} %add.98), channel_id=1, source_target_pairs={{0,128},{64,192},{128,0},{192,64},{1,129},{65,193},{129,1},{193,65... | collective-permute-start | bytes 1228808 | tf_op jit(solution)/shard_map/ppermute | solution.py:75
Sparse Core Ops, SparseCore 0:
  10.4 44.7 all-gather.8
  57.6 43.3 all-gather.4
  176.9 41.8 reduce-scatter.3
  221.1 41.6 reduce-scatter.5
  270.9 26.6 reduce-scatter.7
  331.0 28.9 all-gather.6

commit v6 on v5

--- a/solution.py
+++ b/solution.py
@@ -50,24 +50,18 @@
     return lax.ppermute(block, name, perm=[(0, 1), (1, 0)])
 
 
-def gather_rows(block, prologue):
+def gather_pieces(block, prologue):
     own = lax.all_gather(block, "fx", axis=0, tiled=True)
     partner, prologue = lax.optimization_barrier((swap(block, "fz"), prologue))
+    own_sibling = swap(own, "fc")
     partner = lax.all_gather(partner, "fx", axis=0, tiled=True)
-    block = jnp.concatenate([own, partner], axis=0)
-    return jnp.concatenate([block, swap(block, "fc")], axis=0), prologue
+    partner_sibling = swap(partner, "fc")
+    return (own, partner, own_sibling, partner_sibling), prologue
 
 
-def scatter_rows(block):
-    half = block.shape[0] // 2
-    block = block[:half].astype(jnp.float32) + swap(block[half:], "fc").astype(jnp.float32)
-    block = block.astype(jnp.bfloat16)
-    half = block.shape[0] // 2
-    partner = lax.psum_scatter(block[half:], "fx", scatter_dimension=0, tiled=True)
-    own, partner = lax.optimization_barrier((block[:half], partner))
-    partner = swap(partner, "fz")
-    own = lax.psum_scatter(own, "fx", scatter_dimension=0, tiled=True)
-    return own.astype(jnp.float32) + partner.astype(jnp.float32)
+def fold_core(own, sibling):
+    total = own.astype(jnp.float32) + swap(sibling, "fc").astype(jnp.float32)
+    return total.astype(jnp.bfloat16)
 
 
 def exchange_add(values, name, size, stride):
@@ -112,21 +106,41 @@
     keep_mask = (offsets < lengths[0][:, None]).reshape(frame_rows, 1).astype(jnp.bfloat16)
     masked_grad = cotangent[0] * keep_mask
     prologue = (gathered_order(normed), gathered_order(masked_grad))
-    weights, (normed, masked_grad) = gather_rows(inner_params[0], prologue)
-    w_in = weights[:, 0, :]
-    w_out = weights[:, 1, :]
-    pre_act = jnp.dot(normed, w_in, preferred_element_type=jnp.float32) * model_width ** (-0.5)
-    back_grad = jnp.dot(masked_grad, w_out, preferred_element_type=jnp.float32) * hidden_width ** (-0.5)
+    pieces, (normed, masked_grad) = gather_pieces(inner_params[0], prologue)
+    width = pieces[0].shape[0]
+    normed_parts = [normed[:, i * width : (i + 1) * width] for i in range(len(pieces))]
+    grad_parts = [masked_grad[:, i * width : (i + 1) * width] for i in range(len(pieces))]
+    pre_sum = None
+    back_sum = None
+    for normed_part, grad_part, piece in zip(normed_parts, grad_parts, pieces):
+        pre_term = jnp.dot(normed_part, piece[:, 0, :], preferred_element_type=jnp.float32)
+        back_term = jnp.dot(grad_part, piece[:, 1, :], preferred_element_type=jnp.float32)
+        pre_sum = pre_term if pre_sum is None else pre_sum + pre_term
+        back_sum = back_term if back_sum is None else back_sum + back_term
+    pre_act = pre_sum * model_width ** (-0.5)
+    back_grad = back_sum * hidden_width ** (-0.5)
     activation, derivative = gelu_parts(pre_act)
     activation = activation.astype(jnp.bfloat16)
     hidden_grad = (back_grad * derivative).astype(jnp.bfloat16)
-    grad_in = lax.dot_general(
-        normed, hidden_grad, (((0,), (0,)), ((), ())), preferred_element_type=jnp.float32
-    ) * model_width ** (-0.5)
-    grad_out = lax.dot_general(
-        masked_grad, activation, (((0,), (0,)), ((), ())), preferred_element_type=jnp.float32
-    ) * hidden_width ** (-0.5)
-    gradients = scatter_rows(jnp.stack((grad_in, grad_out), axis=1).astype(jnp.bfloat16))
+
+    def piece_grad(index):
+        grad_in = lax.dot_general(
+            normed_parts[index], hidden_grad, (((0,), (0,)), ((), ())),
+            preferred_element_type=jnp.float32,
+        ) * model_width ** (-0.5)
+        grad_out = lax.dot_general(
+            grad_parts[index], activation, (((0,), (0,)), ((), ())),
+            preferred_element_type=jnp.float32,
+        ) * hidden_width ** (-0.5)
+        return jnp.stack((grad_in, grad_out), axis=1).astype(jnp.bfloat16)
+
+    partner_rows = fold_core(piece_grad(1), piece_grad(3))
+    partner_rows = lax.psum_scatter(partner_rows, "fx", scatter_dimension=0, tiled=True)
+    own_rows = fold_core(piece_grad(0), piece_grad(2))
+    own_rows, partner_rows = lax.optimization_barrier((own_rows, partner_rows))
+    partner_rows = swap(partner_rows, "fz")
+    own_rows = lax.psum_scatter(own_rows, "fx", scatter_dimension=0, tiled=True)
+    gradients = own_rows.astype(jnp.float32) + partner_rows.astype(jnp.float32)
     new_moment = beta_one * first_moment[0] + (1.0 - beta_one) * gradients
     new_second = beta_two * second_moment[0] + (1.0 - beta_two) * gradients * gradients
     update = new_moment / correction_one / (jnp.sqrt(new_second / correction_two) + adam_eps)

time: 378 us -> 354 us (0.937)
  the two profiles are of different devices: /device:TPU:121 before, /device:TPU:1 now
where the time goes in v6:
time: 354 us; the launch traced here: 348 us
  waiting for transfers between devices  208 us (59%)
  matrix products  42.1 us (12%)
  local copies, waits for them, and re-layouts  38 us (11%)
  other arithmetic  25.3 us (7%)
  starting transfers between devices  19.7 us (6%)
  between operations  14.7 us (4%)
    all_gather x1, waiting for transfers between devices, gather_pieces(): partner = lax.all_gather(partner, 'fx', axis=0, tiled=True)  44.6 us
    ppermute x6, waiting for transfers between devices, swap(): return lax.ppermute(block, name, perm=[(0, 1), (1, 0)])  30.2 us
    reduce_scatter x1, waiting for transfers between devices, per_device(): lax.psum_scatter(partner_rows, 'fx', scatter_dimension=0, tiled=True)  28.7 us
    all_gather x1, waiting for transfers between devices, group_sum(): flat = lax.all_gather(flat, 'gy', axis=0, tiled=True)  28.2 us
    reduce_scatter x1, waiting for transfers between devices, group_sum(): flat = lax.psum_scatter(flat, 'gy', scatter_dimension=0, tiled=True)  28 us
    ppermute x2, waiting for transfers between devices, exchange_add(): return values + lax.ppermute(values, name, perm=pairs)  26.5 us
    dot_general x4, matrix products, per_device(): jnp.dot(normed_part, piece[:, 0, :], preferred_element_type=jnp.float32)  17.4 us
    unnamed x50, local copies, waits for them, and re-layouts  15.7 us
  transfers between devices with their start and end apart: 14, of which 11 were waited for; matrix products, arithmetic and copies ran while one was open for 16% of the time, Pallas kernels for 0%

profile of v6, /device:TPU:1, one launch (start us, length us, event | category | flops | bytes accessed | tf_op | source)
XLA Modules:
  0.0 347.9 jit_solution(16835427786748482913)
XLA Ops:
  7.2 2.2 copy.56
  9.5 7.8 %collective-permute-start = (bf16[80,2,2560]{2,0,1:T(8,128)(2,1)}, bf16[80,2,2560]{2,0,1:T(8,128)(2,1)S(1)}, u32[]{:S(2)}, u32[]{:S(2)}) collective-permute-start(bf16[80,2,2560]{2,0,1:T(8,128)(2,1)} %bitcast.115), channel_id=1, source_target_pairs={{0,2},{2,0},{1,3},{3,1},{4,6},{6,4},{5,7},{7,5},{8,10},{10,8},{9,1... | collective-permute-start | bytes 2457608 | tf_op jit(solution)/shard_map/ppermute | solution.py:50
  18.0 1.9 convert_element_type.87
  19.9 1.8 copy.31
  21.7 1.6 copy.35
  23.3 4.0 %gather_fusion = f32[4,128,1280]{2,1,0:T(8,128)} fusion(f32[4,128,1280]{2,1,0:T(8,128)} %bitcast.94, s32[1024]{0:T(1024)S(1)} %pad_clamp_fusion), kind=kCustom, calls=%fused_computation | custom fusion | bytes 5242896 | tf_op jit(solution)/shard_map/jit(_take)/gather | solution.py:102
  27.3 4.2 %copy.32 = f32[4,128,1280]{1,0,2:T(4,128)} copy(f32[4,128,1280]{2,1,0:T(8,128)} %gather_fusion) | data formatting | bytes 5242880 | tf_op jit(solution)/shard_map/jit(_take)/gather | solution.py:102
  31.5 4.1 %gather.9 = f32[512,4,2,2,80]{0,4,3,2,1:T(8,128)} reshape(f32[4,128,1280]{1,0,2:T(4,128)} %copy.32) | data formatting | bytes 5242880 | tf_op jit(solution)/shard_map/jit(_take)/gather | solution.py:102
  35.6 3.3 copy.33
  39.1 2.4 fusion.35
  42.3 1.0 copy-done.2
  43.3 0.8 copy-done.3
  44.1 0.7 multiply_convert_fusion.2
  44.9 0.7 reverse_select_fusion.1
  46.4 1.0 copy-done.19
  47.5 9.9 %all-gather.9.cloned.1.call-done = bf16[1,320,2,2560]{3,1,2,0:T(8,128)(2,1)} async-done(((bf16[1,80,2,2560]{3,1,2,0:T(8,128)(2,1)}), bf16[1,320,2,2560]{3,1,2,0:T(8,128)(2,1)}) %all-gather.9.cloned.1.call-update) | async-done | bytes 3276816 | tf_op jit(solution)/shard_map/all_gather | solution.py:54
  57.4 0.7 collective-permute-start.1
  58.1 44.6 %all-gather.5.cloned.1.call-done = bf16[320,2,2560]{2,0,1:T(8,128)(2,1)} async-done(((bf16[80,2,2560]{2,0,1:T(8,128)(2,1)}), bf16[320,2,2560]{2,0,1:T(8,128)(2,1)}) %all-gather.5.cloned.1.call-update) | async-done | bytes 3276816 | tf_op jit(solution)/shard_map/all_gather | solution.py:57
  102.6 0.9 collective-permute-start.2
  103.6 3.0 fusion.27
  106.6 1.5 fusion.31
  108.2 0.7 copy-done.12
  109.0 1.6 fusion.26
  110.5 1.6 fusion.30
  112.1 5.3 %fusion.25 = f32[512,2560]{1,0:T(8,128)} fusion(bf16[320,2,2560]{2,0,1:T(8,128)(2,1)} %collective-permute-done.1, bf16[512,1280]{0,1:T(8,128)(2,1)S(1)} %bitcast.97), kind=kOutput, calls=%fused_computation.54 | convolution fusion | flops 838860800 | bytes 7208960 | tf_op jit(solution)/shard_map/dot_general | solution.py:116
  117.4 3.0 fusion.29
  120.4 7.5 %multiply_convert_fusion = (bf16[512,2560]{1,0:T(8,128)(2,1)}, f32[512,2560]{1,0:T(8,128)}) fusion(bf16[320,2,2560]{2,0,1:T(8,128)(2,1)} %collective-permute-done.2, bf16[512,1280]{0,1:T(8,128)(2,1)S(1)} %bitcast.98, f32[512,2560]{1,0:T(8,128)} %fusion.25, f32[512,2560]{1,0:T(8,128)S(1)} %fusion.27, f32[512,2560]{1,0:T(8,128)S(1)} %fusion.26), kind=kOutput, calls=%fused_computation.3 | convolution fusion | flops 850657280 | bytes 25559040 | tf_op jit(solution)/shard_map/dot_general | solution.py:116
  127.9 4.1 %fusion.8 = bf16[320,1,2560]{2,0,1:T(8,128)(2,1)} fusion(bf16[512,2560]{1,0:T(8,128)(2,1)} %get-tuple-element.28, bf16[512,1280]{0,1:T(8,128)(2,1)S(1)} %bitcast.107), kind=kOutput, calls=%fused_computation.23 | convolution fusion | flops 840499200 | bytes 4587520 | tf_op jit(solution)/shard_map/dot_general | solution.py:131
  132.0 5.4 %multiply_convert_fusion.1 = bf16[512,2560]{1,0:T(8,128)(2,1)S(1)} fusion(f32[512,2560]{1,0:T(8,128)S(1)} %copy-done.1, f32[512,2560]{1,0:T(8,128)S(1)} %fusion.29, f32[512,2560]{1,0:T(8,128)S(1)} %fusion.31, f32[512,2560]{1,0:T(8,128)S(1)} %fusion.30, bf16[320,2,2560]{2,0,1:T(8,128)(2,1)} %collective-permute-done.2, bf16[512,1280]{0,1:T(8,128)(2,1)} %bitcast.104), kind=kOutput, calls=%fused_computation.4 | convolution fusion | flops 858521600 | bytes 25559040 | tf_op jit(solution)/shard_map/dot_general | solution.py:117
  137.5 1.0 fusion.9
  138.5 1.3 copy-done.17
  140.4 0.8 copy-done.10
  141.2 0.8 copy-done.13
  142.0 1.0 fusion.10
  143.1 1.0 fusion.11
  144.1 2.0 collective-permute-done.4
  146.1 2.6 add_convert_fusion
  148.8 2.9 fusion.12
  151.7 1.0 fusion.13
  153.5 1.0 copy-done.14
  154.5 1.0 fusion.14
  155.5 1.0 fusion.15
  156.6 2.6 collective-permute-done.3
  159.2 2.6 add_convert_fusion.1
  161.8 28.7 %reduce-scatter.4.cloned.1.call-done = bf16[80,2,2560]{2,0,1:T(8,128)(2,1)} async-done(((bf16[320,2,2560]{2,0,1:T(8,128)(2,1)}), bf16[80,2,2560]{2,0,1:T(8,128)(2,1)}) %reduce-scatter.4.cloned.1.call-update) | async-done | bytes 819216 | tf_op jit(solution)/shard_map/reduce_scatter | solution.py:138
  190.6 1.1 copy-done.20
  191.6 5.5 %collective-permute-start.5 = (bf16[80,2,2560]{2,0,1:T(8,128)(2,1)S(1)}, bf16[80,2,2560]{2,0,1:T(8,128)(2,1)}, u32[]{:S(2)}, u32[]{:S(2)}) collective-permute-start(bf16[80,2,2560]{2,0,1:T(8,128)(2,1)S(1)} %copy-done.20), channel_id=1, source_target_pairs={{0,2},{2,0},{1,3},{3,1},{4,6},{6,4},{5,7},{7,5},{8,10},{10,8},{9,1... | collective-permute-start | bytes 2457608 | tf_op jit(solution)/shard_map/ppermute | solution.py:50
  197.1 25.6 %collective-permute-done.5 = bf16[80,2,2560]{2,0,1:T(8,128)(2,1)} collective-permute-done((bf16[80,2,2560]{2,0,1:T(8,128)(2,1)S(1)}, bf16[80,2,2560]{2,0,1:T(8,128)(2,1)}, u32[]{:S(2)}, u32[]{:S(2)}) %collective-permute-start.5) | collective-permute-done | bytes 819232 | tf_op jit(solution)/shard_map/ppermute | solution.py:50
  222.7 11.9 %reduce-scatter.6.cloned.1.call-done = bf16[80,2,2560]{2,0,1:T(8,128)(2,1)} async-done(((bf16[320,2,2560]{2,0,1:T(8,128)(2,1)}), bf16[80,2,2560]{2,0,1:T(8,128)(2,1)}) %reduce-scatter.6.cloned.1.call-update) | async-done | bytes 819216 | tf_op jit(solution)/shard_map/reduce_scatter | solution.py:142
  234.6 4.2 %fusion.18 = (f32[80,2,2560]{2,0,1:T(8,128)S(1)}, f32[1,80,2,2560]{3,1,2,0:T(8,128)S(1)}) fusion(f32[80,2,2560]{2,1,0:T(2,128)S(1)} %copy-done.4, f32[1,80,2,2560]{3,2,1,0:T(2,128)} %param.15, bf16[80,2,2560]{2,0,1:T(8,128)(2,1)} %collective-permute-done.5, bf16[80,2,2560]{2,0,1:T(8,128)(2,1)} %reduce-scatter.6.cloned.1.call-done, ...), kind=kLoop, calls=%fused_computation.45 | loop fusion | flops 7782400 | bytes 10649600 | tf_op jit(solution)/shard_map/sub | solution.py:149
  238.8 1.3 copy.40
  240.1 2.5 reshape.152
  242.7 28.0 %reduce-scatter.8.cloned.1.call-done = f32[800,128]{1,0:T(8,128)} async-done(((f32[3200,128]{1,0:T(8,128)}), f32[800,128]{1,0:T(8,128)}) %reduce-scatter.8.cloned.1.call-update) | async-done | bytes 409616 | tf_op jit(solution)/shard_map/reduce_scatter | solution.py:76
  270.6 1.3 collective-permute-start.6
  271.9 8.9 %collective-permute-done.6 = f32[800,128]{1,0:T(8,128)S(1)} collective-permute-done((f32[800,128]{1,0:T(8,128)}, f32[800,128]{1,0:T(8,128)S(1)}, u32[]{:S(2)}, u32[]{:S(2)}) %collective-permute-start.6) | collective-permute-done | bytes 409632 | tf_op jit(solution)/shard_map/ppermute | solution.py:69
  280.8 1.1 add.126
  281.9 2.6 collective-permute-start.7
  284.5 17.6 %collective-permute-done.7 = f32[800,128]{1,0:T(8,128)S(1)} collective-permute-done((f32[800,128]{1,0:T(8,128)S(1)}, f32[800,128]{1,0:T(8,128)S(1)}, u32[]{:S(2)}, u32[]{:S(2)}) %collective-permute-start.7) | collective-permute-done | bytes 409632 | tf_op jit(solution)/shard_map/ppermute | solution.py:69
  302.1 0.8 add.127
  302.9 2.4 copy.41
  305.3 28.2 %all-gather.7.cloned.1.call-done = f32[3200,128]{1,0:T(8,128)} async-done(((f32[800,128]{1,0:T(8,128)}), f32[3200,128]{1,0:T(8,128)}) %all-gather.7.cloned.1.call-update) | async-done | bytes 1638416 | tf_op jit(solution)/shard_map/all_gather | solution.py:81
  333.5 1.5 broadcast_multiply_fusion
  335.1 0.9 mul.222
  336.0 4.8 %multiply_subtract_fusion = (f32[80,2,2560]{2,1,0:T(2,128)}, f32[80,2,2560]{2,1,0:T(2,128)}) fusion(f32[80,2,2560]{2,1,0:T(2,128)} %param.16, f32[80,2,2560]{2,1,0:T(2,128)S(1)} %mul.222, f32[80,2,2560]{2,1,0:T(2,128)} %param.17), kind=kLoop, calls=%fused_computation.70 | loop fusion | flops 2457600 | bytes 8192000 | tf_op jit(solution)/shard_map/sub | solution.py:156
  (70 shorter events, 3.9 us)
Async XLA Ops:
  7.2 10.2 %copy-start.18 = (bf16[1,512,1280]{2,1,0:T(8,128)(2,1)S(1)}, bf16[1,512,1280]{2,1,0:T(8,128)(2,1)}, u32[]{:S(2)}) copy-start(bf16[1,512,1280]{2,1,0:T(8,128)(2,1)} %param.9) | copy-start | bytes 3932164
  7.2 50.2 %all-gather.9.cloned.1.call-start = ((), (), s32[]{:S(2)}) async-start(), calls=%async_computation.8 | async-start | bytes 4096000 | tf_op jit(solution)/shard_map/all_gather | solution.py:54
  9.5 93.2 %all-gather.5.cloned.1.call-start = ((), (), s32[]{:S(2)}) async-start(), calls=%async_computation.3 | async-start | bytes 4096000 | tf_op jit(solution)/shard_map/all_gather | solution.py:57
  9.5 36.9 %collective-permute-start = (bf16[80,2,2560]{2,0,1:T(8,128)(2,1)}, bf16[80,2,2560]{2,0,1:T(8,128)(2,1)S(1)}, u32[]{:S(2)}, u32[]{:S(2)}) collective-permute-start(bf16[80,2,2560]{2,0,1:T(8,128)(2,1)} %bitcast.115), channel_id=1, source_target_pairs={{0,2},{2,0},{1,3},{3,1},{4,6},{6,4},{5,7},{7,5},{8,10},{10,8},{9,1... | collective-permute-start | bytes 2457608 | tf_op jit(solution)/shard_map/ppermute | solution.py:50
  19.8 3.4 copy-start.21
  35.6 3.4 copy-start.22
  39.0 2.6 copy-start
  41.5 1.8 copy-start.2
  41.5 2.6 copy-start.3
  46.0 57.6 %copy-start.5 = (bf16[512,2,2,4,80]{0,4,3,2,1:T(8,128)(2,1)}, bf16[512,2,2,4,80]{0,4,3,2,1:T(8,128)(2,1)S(1)}, u32[]{:S(2)}) copy-start(bf16[512,2,2,4,80]{0,4,3,2,1:T(8,128)(2,1)S(1)} %copy.34) | copy-start | bytes 3932164
  46.4 60.3 %copy-start.8 = (bf16[512,2,2,4,80]{0,4,3,2,1:T(8,128)(2,1)}, bf16[512,2,2,4,80]{0,4,3,2,1:T(8,128)(2,1)S(1)}, u32[]{:S(2)}) copy-start(bf16[512,2,2,4,80]{0,4,3,2,1:T(8,128)(2,1)S(1)} %copy.36) | copy-start | bytes 3932164
  46.4 1.0 copy-start.19
  47.4 143.1 %reduce-scatter.4.cloned.1.call-start = ((), (), s32[]{:S(2)}) async-start(), calls=%async_computation.4 | async-start | bytes 4096000 | tf_op jit(solution)/shard_map/reduce_scatter | solution.py:138
  57.4 54.7 %collective-permute-start.1 = (bf16[320,2,2560]{2,0,1:T(8,128)(2,1)}, bf16[320,2,2560]{2,0,1:T(8,128)(2,1)}, u32[]{:S(2)}, u32[]{:S(2)}) collective-permute-start(bf16[320,2,2560]{2,0,1:T(8,128)(2,1)} %bitcast.112), channel_id=1, source_target_pairs={{0,1},{1,0},{2,3},{3,2},{4,5},{5,4},{6,7},{7,6},{8,9},{9,8},{10,11... | collective-permute-start | bytes 9830408 | tf_op jit(solution)/shard_map/ppermute | solution.py:50
  102.6 4.0 %copy-start.11 = (bf16[1,320,2,2560]{3,1,2,0:T(8,128)(2,1)S(1)}, bf16[1,320,2,2560]{3,1,2,0:T(8,128)(2,1)}, u32[]{:S(2)}) copy-start(bf16[1,320,2,2560]{3,1,2,0:T(8,128)(2,1)} %all-gather.9.cloned.1.call-done) | copy-start | bytes 9830404
  102.6 17.8 %collective-permute-start.2 = (bf16[320,2,2560]{2,0,1:T(8,128)(2,1)}, bf16[320,2,2560]{2,0,1:T(8,128)(2,1)}, u32[]{:S(2)}, u32[]{:S(2)}) collective-permute-start(bf16[320,2,2560]{2,0,1:T(8,128)(2,1)} %all-gather.5.cloned.1.call-done), channel_id=1, source_target_pairs={{0,1},{1,0},{2,3},{3,2},{4,5},{5,4},{6,7},{7,6},{8,9},{9,8},{10,11... | collective-permute-start | bytes 9830408 | tf_op jit(solution)/shard_map/ppermute | solution.py:50
  106.6 1.6 copy-start.6
  106.6 2.3 copy-start.12
  109.0 1.6 copy-start.9
  127.9 4.1 %copy-start.1 = (f32[512,2560]{1,0:T(8,128)S(1)}, f32[512,2560]{1,0:T(8,128)}, u32[]{:S(2)}) copy-start(f32[512,2560]{1,0:T(8,128)} %get-tuple-element.29) | copy-start | bytes 15728644
  132.0 5.4 %copy-start.7 = (bf16[512,2,2,4,80]{0,4,3,2,1:T(8,128)(2,1)S(1)}, bf16[512,2,2,4,80]{0,4,3,2,1:T(8,128)(2,1)}, u32[]{:S(2)}) copy-start(bf16[512,2,2,4,80]{0,4,3,2,1:T(8,128)(2,1)} %copy-done.5) | copy-start | bytes 3932164
  137.5 5.6 %copy-start.15 = (bf16[512,2560]{1,0:T(8,128)(2,1)}, bf16[512,2560]{1,0:T(8,128)(2,1)S(1)}, u32[]{:S(2)}) copy-start(bf16[512,2560]{1,0:T(8,128)(2,1)S(1)} %multiply_convert_fusion.1) | copy-start | bytes 7864324
  137.5 2.4 copy-start.17
  139.9 1.3 copy-start.10
  139.9 2.1 copy-start.13
  140.2 5.9 %collective-permute-start.4 = (bf16[320,2,2560]{2,0,1:T(8,128)(2,1)S(1)}, bf16[320,2,2560]{2,0,1:T(8,128)(2,1)S(1)}, u32[]{:S(2)}, u32[]{:S(2)}) collective-permute-start(bf16[320,2,2560]{2,0,1:T(8,128)(2,1)S(1)} %pad_maximum_fusion.1), channel_id=1, source_target_pairs={{0,1},{1,0},{2,3},{3,2},{4,5},{5,4},{6,7},{7,6},{8,9},{9,8},{10,11... | collective-permute-start | bytes 9830408 | tf_op jit(solution)/shard_map/ppermute | solution.py:50
  148.7 85.9 %reduce-scatter.6.cloned.1.call-start = ((), (), s32[]{:S(2)}) async-start(), calls=%async_computation.5 | async-start | bytes 4096000 | tf_op jit(solution)/shard_map/reduce_scatter | solution.py:142
  148.8 2.9 copy-start.16
  152.7 1.7 copy-start.14
  153.1 6.1 %collective-permute-start.3 = (bf16[320,2,2560]{2,0,1:T(8,128)(2,1)S(1)}, bf16[320,2,2560]{2,0,1:T(8,128)(2,1)S(1)}, u32[]{:S(2)}, u32[]{:S(2)}) collective-permute-start(bf16[320,2,2560]{2,0,1:T(8,128)(2,1)S(1)} %pad_maximum_fusion), channel_id=1, source_target_pairs={{0,1},{1,0},{2,3},{3,2},{4,5},{5,4},{6,7},{7,6},{8,9},{9,8},{10,11... | collective-permute-start | bytes 9830408 | tf_op jit(solution)/shard_map/ppermute | solution.py:50
  161.8 72.8 %copy-start.4 = (f32[80,2,2560]{2,1,0:T(2,128)S(1)}, f32[80,2,2560]{2,1,0:T(2,128)}, u32[]{:S(2)}) copy-start(f32[80,2,2560]{2,1,0:T(2,128)} %param.16) | copy-start | bytes 4915204
  190.5 1.1 copy-start.20
  190.5 80.1 %reduce-scatter.8.cloned.1.call-start = ((), (), s32[]{:S(2)}) async-start(), calls=%async_computation.6 | async-start | bytes 2048000 | tf_op jit(solution)/shard_map/reduce_scatter | solution.py:76
  191.6 31.0 %collective-permute-start.5 = (bf16[80,2,2560]{2,0,1:T(8,128)(2,1)S(1)}, bf16[80,2,2560]{2,0,1:T(8,128)(2,1)}, u32[]{:S(2)}, u32[]{:S(2)}) collective-permute-start(bf16[80,2,2560]{2,0,1:T(8,128)(2,1)S(1)} %copy-done.20), channel_id=1, source_target_pairs={{0,2},{2,0},{1,3},{3,1},{4,6},{6,4},{5,7},{7,5},{8,10},{10,8},{9,1... | collective-permute-start | bytes 2457608 | tf_op jit(solution)/shard_map/ppermute | solution.py:50
  242.6 90.9 %all-gather.7.cloned.1.call-start = ((), (), s32[]{:S(2)}) async-start(), calls=%async_computation.7 | async-start | bytes 2048000 | tf_op jit(solution)/shard_map/all_gather | solution.py:81
  270.6 10.2 %collective-permute-start.6 = (f32[800,128]{1,0:T(8,128)}, f32[800,128]{1,0:T(8,128)S(1)}, u32[]{:S(2)}, u32[]{:S(2)}) collective-permute-start(f32[800,128]{1,0:T(8,128)} %reduce-scatter.8.cloned.1.call-done), channel_id=1, source_target_pairs={{0,64},{64,0},{128,192},{192,128},{1,65},{65,1},{129,193},{193,129... | collective-permute-start | bytes 1228808 | tf_op jit(solution)/shard_map/ppermute | solution.py:69
  281.9 20.2 %collective-permute-start.7 = (f32[800,128]{1,0:T(8,128)S(1)}, f32[800,128]{1,0:T(8,128)S(1)}, u32[]{:S(2)}, u32[]{:S(2)}) collective-permute-start(f32[800,128]{1,0:T(8,128)S(1)} %add.126), channel_id=1, source_target_pairs={{0,128},{64,192},{128,0},{192,64},{1,129},{65,193},{129,1},{193,65... | collective-permute-start | bytes 1228808 | tf_op jit(solution)/shard_map/ppermute | solution.py:69
Sparse Core Ops, SparseCore 0:
  10.4 46.9 all-gather.8
  59.2 43.3 all-gather.4
  148.8 41.6 reduce-scatter.3
  192.9 41.6 reduce-scatter.5
  242.7 27.8 reduce-scatter.7
  303.0 30.4 all-gather.6
